TPU v7x, 256 devices: a whole 4x4x8 slice. The times are simulated.
256 devices in a mesh: gx: 8 (over z), gz: 8 (over y, core), row: 4 (over x).
Axes of the slice: x: 4, y: 4, z: 8, core: 2. Of those that a mesh axis runs over, the one named last changes fastest.
Arguments:
- flow_field: float32 [5, 32, 256, 512], P(None, 'gx', 'gz', 'row'), may hold values from -6 to 6
- flux_jacobian: float32 [3, 5, 5], replicated, may hold values from -2.5 to 2.5
- history: float32 [98304, 5, 128], P(('gx', 'gz', 'row')), may hold values from -6 to 6
- surface_cell: int32 [1536, 64], P(('gx', 'gz', 'row')), may hold values from 0 to 16383
- surface_blocks: int32 [4, 64], P('row', ('gx', 'gz')), may hold values from 1 to 6, 128 in all within a row
- observers: float32 [3, 256], replicated, may hold values from 0 to 1
Outputs:
- field_out: float32 [5, 32, 256, 512], P(None, 'gx', 'gz', 'row')
- spectrum: float32 [256, 64], P(('gx', 'gz', 'row'))
Inputs may be any that keep to these rules, and one draw needn't show every extreme that they name: The patch with index g of gx+gz and index q of row has exactly 64 * surface_blocks[q, g] live slots, its first ones.
All inputs are finite; a program needn't handle non-finite values. No bound on the sum of `surface_blocks` on one device may be relied on, other than what follows from the above.
Results may differ from a plain program's by a relative error of at most 0.0003.
Values sent between devices are 32-bit elements; how exact they have to be, the bound alone decides.
A program may use at most 64 MiB of HBM per device.

v0:
```python
import math

import jax
import jax.numpy as jnp
from jax import lax
from jax.sharding import Mesh
from jax.sharding import PartitionSpec as P

SURF_DEV = 128
FREQ = 32
STEPS = 3
GZ = ("gz_0", "gz_1")
GX_GZ_ROW = ("gx", "gz_0", "gz_1", "row")
GX_GZ = ("gx", "gz_0", "gz_1")


TIME_STEP = 0.3
VISCOSITY = 0.05


def padded_2(value, sides, width):
    for axis, dim in sides:
        peers, length = (lax.axis_size(axis), value.shape[dim])
        up = [(i, (i + 1) % peers) for i in range(peers - 1)]
        down = [(j, i) for i, j in up]
        last = lax.slice_in_dim(value, length - width, length, axis=dim)
        leading = lax.slice_in_dim(value, 0, width, axis=dim)
        before = lax.ppermute(last, axis, up)
        after = lax.ppermute(leading, axis, down)
        value = jnp.concatenate([before, value, after], axis=dim)
    return value


def reduced_to_own(tiles, axes, order):
    shape = [lax.axis_size(a) for a in axes]
    tiles = tiles.reshape(*shape, *tiles.shape[1:])
    tiles = tiles.transpose(*order, *range(len(axes), tiles.ndim))
    tiles = tiles.reshape(-1, *tiles.shape[len(axes) :])
    for k in order:
        tiles = lax.psum_scatter(tiles, axes[k], scatter_dimension=0, tiled=True)
    return tiles[0]


def split_up(value, dim, peers):
    before, after = (value.shape[:dim], value.shape[dim + 1 :])
    return jnp.moveaxis(value.reshape(*before, peers, -1, *after), dim, 0)


def scatter_axes(value, axes, order, dim):
    peers = lax.axis_size(axes)
    return reduced_to_own(split_up(value, dim, peers), axes, order)


def stencil_rate(padded, flux_jacobian):
    center = padded[:, 1:-1, 1:-1, 1:-1]
    along_x = (padded[:, 2:, 1:-1, 1:-1] - padded[:, :-2, 1:-1, 1:-1]) * 0.5
    along_z = (padded[:, 1:-1, 2:, 1:-1] - padded[:, 1:-1, :-2, 1:-1]) * 0.5
    along_r = (padded[:, 1:-1, 1:-1, 2:] - padded[:, 1:-1, 1:-1, :-2]) * 0.5
    beside = padded[:, 2:, 1:-1, 1:-1] + padded[:, :-2, 1:-1, 1:-1]
    beside = beside + padded[:, 1:-1, 2:, 1:-1] + padded[:, 1:-1, :-2, 1:-1]
    beside = beside + padded[:, 1:-1, 1:-1, 2:] + padded[:, 1:-1, 1:-1, :-2]
    slopes = jnp.stack([along_x, along_z, along_r])
    transport = jnp.einsum(
        "dvw,dwxzr->vxzr", flux_jacobian, slopes, precision=lax.Precision.HIGHEST
    )
    return transport + VISCOSITY * (beside - 6.0 * center)


def fourier_table(samples, freq_count):
    time_ids = jnp.arange(samples, dtype=jnp.int32)
    freq_ids = jnp.arange(1, freq_count + 1, dtype=jnp.int32)
    turn_ids = freq_ids[:, None] * time_ids[None, :] % samples
    angles = 2.0 * math.pi / samples * turn_ids.astype(jnp.float32)
    norm_scale = 1.0 / math.sqrt(samples)
    return jnp.concatenate([jnp.cos(angles), -jnp.sin(angles)], axis=0) * norm_scale


def spectra_of(signals, fourier):
    return jnp.einsum("ft,svt->vfs", fourier, signals, precision=lax.Precision.HIGHEST)


def radiate(points, monopole, dipole, watchers, radial_cells, freq_count):
    wavenumbers = jnp.arange(1, freq_count + 1, dtype=jnp.float32) * (2.0 / radial_cells)
    offset_vec = watchers[:, :, None] - points[None, :, :]
    distance = jnp.sqrt(jnp.sum(offset_vec * offset_vec, axis=1))
    direction = offset_vec / distance[:, None, :]
    amplitude = (radial_cells / distance)[:, None, :]
    dip_real = direction[:, 0, None, :] * dipole[0, None, :freq_count, :]
    dip_real = dip_real + direction[:, 1, None, :] * dipole[1, None, :freq_count, :]
    dip_real = dip_real + direction[:, 2, None, :] * dipole[2, None, :freq_count, :]
    dip_imag = direction[:, 0, None, :] * dipole[0, None, freq_count:, :]
    dip_imag = dip_imag + direction[:, 1, None, :] * dipole[1, None, freq_count:, :]
    dip_imag = dip_imag + direction[:, 2, None, :] * dipole[2, None, freq_count:, :]
    mono_real = monopole[None, :freq_count, :]
    mono_imag = monopole[None, freq_count:, :]
    phase_arg = distance[:, None, :] * wavenumbers[None, :, None]
    near_term = 1.0 / phase_arg
    cosine = amplitude * jnp.cos(phase_arg)
    sine = amplitude * jnp.sin(phase_arg)
    plus_weight = cosine * near_term + sine
    minus_weight = cosine - sine * near_term
    out_real = jnp.sum(
        plus_weight * dip_real - minus_weight * dip_imag + sine * mono_real - cosine * mono_imag,
        axis=2,
    )
    out_imag = jnp.sum(
        minus_weight * dip_real + plus_weight * dip_imag + cosine * mono_real + sine * mono_imag,
        axis=2,
    )
    return jnp.concatenate([out_real, out_imag], axis=1)


def per_device(flow_field, flux_jacobian, history, surface_cell, surface_blocks, observers):
    width_x, width_z, width_r = (flow_field.shape[1], flow_field.shape[2], flow_field.shape[3])
    count_x, count_z, count_r = (lax.axis_size("gx"), lax.axis_size(GZ), lax.axis_size("row"))
    index_x, index_z, index_r = (lax.axis_index("gx"), lax.axis_index(GZ), lax.axis_index("row"))
    owners = count_x * count_z
    devices = owners * count_r
    radial_cells = width_r * count_r
    slot_rows = surface_cell.shape[0]
    capacity = slot_rows * owners
    samples = history.shape[2]
    cell_ids = surface_cell.reshape(-1)

    def inside_mask(margin):
        coord_x = index_x * width_x + jnp.arange(width_x + 2 * margin, dtype=jnp.int32) - margin
        coord_z = index_z * width_z + jnp.arange(width_z + 2 * margin, dtype=jnp.int32) - margin
        coord_r = index_r * width_r + jnp.arange(width_r + 2 * margin, dtype=jnp.int32) - margin
        valid_x = (coord_x >= 0) & (coord_x < width_x * count_x)
        valid_z = (coord_z >= 0) & (coord_z < width_z * count_z)
        valid_r = (coord_r >= 0) & (coord_r < radial_cells)
        joined = valid_x[:, None, None] & valid_z[None, :, None] & valid_r[None, None, :]
        return joined.astype(jnp.float32)[None]

    mask_outer = inside_mask(2)
    mask_inner = inside_mask(1)
    current = flow_field
    sampled = []
    for step_index in range(STEPS):
        extended = padded_2(current, (("gx", 1), (GZ, 2), ("row", 3)), 3)
        section_one = (
            extended[:, 1:-1, 1:-1, 1:-1] + TIME_STEP * stencil_rate(extended, flux_jacobian)
        ) * mask_outer
        section_two = 0.75 * extended[:, 2:-2, 2:-2, 2:-2] + 0.25 * (
            section_one[:, 1:-1, 1:-1, 1:-1] + TIME_STEP * stencil_rate(section_one, flux_jacobian)
        )
        section_two = section_two * mask_inner
        current = extended[:, 3:-3, 3:-3, 3:-3] / 3.0 + 2.0 / 3.0 * (
            section_two[:, 1:-1, 1:-1, 1:-1] + TIME_STEP * stencil_rate(section_two, flux_jacobian)
        )
        sampled.append(jnp.take(current.reshape(5, -1), cell_ids, axis=1))
    recent = jnp.transpose(jnp.stack(sampled, axis=2), (1, 0, 2))
    signals = jnp.concatenate([history[:, :, : samples - STEPS], recent], axis=2)
    global_x = index_x * width_x + cell_ids // (width_z * width_r)
    global_z = index_z * width_z + cell_ids // width_r % width_z
    global_r = index_r * width_r + cell_ids % width_r
    positions = jnp.stack([global_x, global_z, global_r]).astype(jnp.float32) + 0.5
    fourier = fourier_table(samples, FREQ)
    live_mask = (jnp.arange(capacity, dtype=jnp.int32) // owners < surface_blocks[0, 0]).astype(
        jnp.float32
    )
    spectra = spectra_of(signals, fourier) * live_mask
    monopole = spectra[0] + spectra[4]
    dipole = spectra[1:4]
    watchers = jnp.stack(
        [
            observers[0] * (width_x * count_x),
            observers[1] * (width_z * count_z),
            (1.25 + 0.75 * observers[2]) * radial_cells,
        ],
        axis=1,
    )
    norm_scale = math.sqrt(devices * SURF_DEV)
    row_count = observers.shape[1] // devices * lax.axis_size(GX_GZ_ROW)
    block_size = math.gcd(row_count, 32)

    def one_block(block):
        return radiate(positions, monopole, dipole, block, radial_cells, FREQ)

    blocks_out = lax.map(one_block, watchers.reshape(row_count // block_size, block_size, 3))
    spectrum = scatter_axes(
        blocks_out.reshape(row_count, 2 * FREQ) / norm_scale, GX_GZ_ROW, (2, 0, 1, 3), 0
    )
    return (current, spectrum)


def solution(mesh):
    finer = Mesh(
        mesh.devices.reshape(mesh.shape["gx"], 4, 2, mesh.shape["row"]),
        ("gx", "gz_0", "gz_1", "row"),
    )
    return jax.shard_map(
        per_device,
        mesh=finer,
        in_specs=(
            P(None, "gx", GZ, "row"),
            P(),
            P(GX_GZ_ROW, None, None),
            P(GX_GZ_ROW, None),
            P("row", GX_GZ),
            P(),
        ),
        out_specs=(P(None, "gx", GZ, "row"), P(GX_GZ_ROW, None)),
        check_vma=False,
    )
```

profile of v0, /device:TPU:32, one launch (start us, length us, event | category | flops | bytes accessed | tf_op | source)
XLA Modules:
  0.0 416.6 jit_solution(16389167515015480363)
XLA Ops:
  8.5 3.8 collective-permute-start
  12.5 2.7 collective-permute-start.1
  16.6 4.8 %collective-permute-done = f32[5,3,32,128]{3,0,2,1:T(8,128)} collective-permute-done((f32[5,3,32,128]{3,0,2,1:T(8,128)S(1)}, f32[5,3,32,128]{3,0,2,1:T(8,128)}, u32[]{:S(2)}, u32[]{:S(2)}) %collective-permute-start) | collective-permute-done | bytes 245792 | tf_op jit(solution)/shard_map/ppermute | solution.py:28
  22.6 2.5 collective-permute-done.1
  28.4 3.1 collective-permute-done.3
  35.9 4.0 collective-permute-start.4
  45.4 2.6 collective-permute-done.5
  47.9 2.7 copy.135
  50.7 2.7 pad_maximum_fusion.5
  53.4 3.1 multiply_bitcast_fusion.8
  56.5 8.4 %fusion.36 = f32[5,8,36,132]{3,0,2,1:T(8,128)S(1)} fusion(f32[5,10,38,134]{3,0,2,1:T(8,128)S(1)} %pad_maximum_fusion.5, f32[1,5,8,36,132]{4,1,0,3,2:T(8,128)S(1)} %get-tuple-element.83, f32[1,5,8,36,132]{4,1,0,3,2:T(8,128)S(1)} %get-tuple-element.84, f32[1,5,8,36,132]{4,1,0,3,2:T(8,128)S(1)} %get-tuple-element.82, f32[8,36,132]{2,1,0:T(8,128)S(1)} %copy-done.4, ...), kind=kOutput, calls=%fused_computation.68 | convolution fusion | flops 37635840 | bytes 8515884 | tf_op jit(solution)/shard_map/dvw,dwxzr->vxzr/dot_general | solution.py:63
  65.0 2.2 multiply_bitcast_fusion.17
  67.2 3.8 fusion.72
  71.0 3.3 fusion.56
  77.1 5.0 %collective-permute-start.6 = (f32[5,3,32,128]{3,0,2,1:T(8,128)S(1)}, f32[5,3,32,128]{3,0,2,1:T(8,128)S(1)}, u32[]{:S(2)}, u32[]{:S(2)}) collective-permute-start(f32[5,3,32,128]{3,0,2,1:T(8,128)S(1)} %get-tuple-element.117), channel_id=1, source_target_pairs={{0,32},{32,64},{64,96},{96,128},{128,160},{160,192},{192,224},{1,3... | collective-permute-start | bytes 737288 | tf_op jit(solution)/shard_map/ppermute | solution.py:28
  84.5 6.1 %collective-permute-done.6 = f32[5,3,32,128]{3,0,2,1:T(8,128)S(1)} collective-permute-done((f32[5,3,32,128]{3,0,2,1:T(8,128)S(1)}, f32[5,3,32,128]{3,0,2,1:T(8,128)S(1)}, u32[]{:S(2)}, u32[]{:S(2)}) %collective-permute-start.6) | collective-permute-done | bytes 245792 | tf_op jit(solution)/shard_map/ppermute | solution.py:28
  90.6 5.3 %collective-permute-done.7 = f32[5,3,32,128]{3,0,2,1:T(8,128)S(1)} collective-permute-done((f32[5,3,32,128]{3,0,2,1:T(8,128)S(1)}, f32[5,3,32,128]{3,0,2,1:T(8,128)S(1)}, u32[]{:S(2)}, u32[]{:S(2)}) %collective-permute-start.7) | collective-permute-done | bytes 245792 | tf_op jit(solution)/shard_map/ppermute | solution.py:29
  95.9 2.8 collective-permute-start.8
  100.8 4.1 collective-permute-done.9
  108.6 3.4 collective-permute-start.10
  116.6 3.4 collective-permute-done.11
  120.0 2.7 copy.148
  122.8 2.7 pad_maximum_fusion.6
  125.4 3.1 multiply_bitcast_fusion.5
  128.6 5.4 %fusion.45 = f32[8,36,132,5]{2,3,0,1:T(8,128)S(1)} fusion(f32[3,5,5,1,1]{2,0,1,4,3:T(4,128)S(1)} %bitcast.244, f32[1,5,8,36,132]{4,1,3,2,0:T(8,128)S(1)} %get-tuple-element.80, f32[1,5,8,36,132]{4,1,3,2,0:T(8,128)S(1)} %get-tuple-element.81, f32[1,5,8,36,132]{4,1,3,2,0:T(8,128)S(1)} %get-tuple-element.79), kind=kOutput, calls=%fused_computation.86 | convolution fusion | flops 35354880 | bytes 3041580 | tf_op jit(solution)/shard_map/dvw,dwxzr->vxzr/dot_general | solution.py:63
  134.0 4.3 %fusion.42 = f32[5,8,36,132]{3,0,2,1:T(8,128)S(1)} fusion(f32[8,36,132,5]{2,3,0,1:T(8,128)S(1)} %fusion.45, f32[5,10,38,134]{3,0,2,1:T(8,128)S(1)} %pad_maximum_fusion.6, f32[8,36,132]{2,1,0:T(8,128)S(1)} %copy-done.5), kind=kLoop, calls=%fused_computation.76 | loop fusion | flops 2280960 | bytes 6994944 | tf_op jit(solution)/shard_map/mul | solution.py:141
  140.5 3.8 fusion.75
  144.3 3.3 fusion.54
  150.4 3.6 collective-permute-start.12
  154.1 2.4 collective-permute-start.13
  157.9 5.3 %collective-permute-done.12 = f32[5,3,32,128]{3,0,2,1:T(8,128)S(1)} collective-permute-done((f32[5,3,32,128]{3,0,2,1:T(8,128)S(1)}, f32[5,3,32,128]{3,0,2,1:T(8,128)S(1)}, u32[]{:S(2)}, u32[]{:S(2)}) %collective-permute-start.12) | collective-permute-done | bytes 245792 | tf_op jit(solution)/shard_map/ppermute | solution.py:28
  163.2 4.0 collective-permute-done.13
  167.2 2.5 collective-permute-start.14
  171.1 4.6 %collective-permute-done.15 = f32[5,10,3,128]{3,0,2,1:T(8,128)S(1)} collective-permute-done((f32[5,10,3,128]{3,0,2,1:T(8,128)S(1)}, f32[5,10,3,128]{3,0,2,1:T(8,128)S(1)}, u32[]{:S(2)}, u32[]{:S(2)}) %collective-permute-start.15) | collective-permute-done | bytes 76832 | tf_op jit(solution)/shard_map/ppermute | solution.py:29
  180.0 3.1 collective-permute-start.16
  186.1 5.3 %copy.171 = f32[5,16384]{0,1:T(8,128)} copy(f32[5,16384]{1,0:T(8,128)S(1)} %bitcast.246) | data formatting | bytes 655360 | tf_op jit(solution)/shard_map/reshape | solution.py:151
  191.4 5.0 %gather_fusion = f32[384,5]{1,0:T(8,128)} fusion(f32[5,16384]{0,1:T(8,128)} %copy.171, s32[1024]{0:T(1024)S(1)} %pad_clamp_fusion), kind=kCustom, calls=%fused_computation.clone | custom fusion | bytes 16896 | tf_op jit(solution)/shard_map/jit(_take)/gather | solution.py:151
  196.4 5.3 %copy.173 = f32[5,16384]{0,1:T(8,128)} copy(f32[5,16384]{1,0:T(8,128)S(1)} %bitcast.247) | data formatting | bytes 655360 | tf_op jit(solution)/shard_map/reshape | solution.py:151
  201.6 5.0 %gather_fusion.1 = f32[384,5]{1,0:T(8,128)} fusion(f32[5,16384]{0,1:T(8,128)} %copy.173, s32[1024]{0:T(1024)S(1)} %pad_clamp_fusion), kind=kCustom, calls=%fused_computation.1.clone | custom fusion | bytes 16896 | tf_op jit(solution)/shard_map/jit(_take)/gather | solution.py:151
  208.3 2.7 copy.161
  211.0 2.7 pad_maximum_fusion.7
  213.7 4.5 %multiply_bitcast_fusion.2 = (f32[1,5,8,36,132]{4,1,3,2,0:T(8,128)S(1)}, f32[1,5,8,36,132]{4,1,3,2,0:T(8,128)S(1)}, f32[1,5,8,36,132]{4,1,3,2,0:T(8,128)}) fusion(f32[5,10,38,134]{3,0,2,1:T(8,128)S(1)} %pad_maximum_fusion.7), kind=kLoop, calls=%fused_computation.79 | loop fusion | flops 1140480 | bytes 6842880 | tf_op jit(solution)/shard_map/stack | solution.py:62
  218.2 7.3 %fusion.48 = f32[8,36,132,5]{2,3,0,1:T(8,128)S(1)} fusion(f32[3,5,5,1,1]{2,0,1,4,3:T(4,128)S(1)} %bitcast.241, f32[1,5,8,36,132]{4,1,3,2,0:T(8,128)S(1)} %get-tuple-element.77, f32[1,5,8,36,132]{4,1,3,2,0:T(8,128)} %get-tuple-element.78, f32[1,5,8,36,132]{4,1,3,2,0:T(8,128)S(1)} %get-tuple-element.76), kind=kOutput, calls=%fused_computation.87 | convolution fusion | flops 35354880 | bytes 3041580 | tf_op jit(solution)/shard_map/dvw,dwxzr->vxzr/dot_general | solution.py:63
  225.5 4.2 %fusion.39 = f32[5,8,36,132]{3,0,2,1:T(8,128)S(1)} fusion(f32[8,36,132,5]{2,3,0,1:T(8,128)S(1)} %fusion.48, f32[5,10,38,134]{3,0,2,1:T(8,128)S(1)} %pad_maximum_fusion.7, f32[8,36,132]{2,1,0:T(8,128)S(1)} %copy-done.6), kind=kLoop, calls=%fused_computation.72 | loop fusion | flops 2280960 | bytes 6994944 | tf_op jit(solution)/shard_map/mul | solution.py:141
  231.9 3.8 fusion.78
  235.7 3.3 fusion.52
  241.8 5.6 %copy.175 = f32[5,16384]{0,1:T(8,128)} copy(f32[5,16384]{1,0:T(8,128)S(1)} %bitcast.248) | data formatting | bytes 655360 | tf_op jit(solution)/shard_map/reshape | solution.py:151
  247.4 4.5 %gather_fusion.2 = f32[384,5]{1,0:T(8,128)S(1)} fusion(f32[5,16384]{0,1:T(8,128)} %copy.175, s32[1024]{0:T(1024)S(1)} %pad_clamp_fusion), kind=kCustom, calls=%fused_computation.2.clone | custom fusion | bytes 16896 | tf_op jit(solution)/shard_map/jit(_take)/gather | solution.py:151
  252.7 2.9 copy.177
  255.6 2.9 copy.178
  258.5 3.8 copy.179
  265.0 69.9 %while.10 = (s32[]{:T(128)}, f32[8,32,64]{2,1,0:T(8,128)S(1)}, f32[8,32,3]{1,2,0:T(4,128)}, f32[3,384]{1,0:T(4,128)S(1)}, f32[3,64,384]{2,1,0:T(8,128)S(1)}, /*index=5*/f32[64,384]{1,0:T(8,128)S(1)}, s32[]{:T(128)}) while((s32[]{:T(128)}, f32[8,32,64]{2,1,0:T(8,128)S(1)}, f32[8,32,3]{1,2,0:T(4,128)}, f32[3,384]{1,0:T(4,128)S(1)}, ...), condition=%wide.region_4.6_spmd, body=%wide.region_0.5_spmd.sunk | while | flops 13553730 | bytes 2181973 | solution.py:180
  266.0 7.7 %fusion.154 = (f32[32,32]{1,0:T(8,128)S(1)}, f32[32,32]{1,0:T(8,128)S(1)}) fusion(f32[32,384]{1,0:T(8,128)S(1)} %get-tuple-element.181, f32[32,384]{1,0:T(8,128)S(1)} %get-tuple-element.182, f32[32,384]{1,0:T(8,128)S(1)} %get-tuple-element.183, f32[32,384]{1,0:T(8,128)S(1)} %get-tuple-element.184, f32[32,384]{1,0:T(8,128)S(1)} %get-tuple-element.185, ...), kind=kLoop, calls=%fused_computation.13.clone.1 | loop fusion | flops 13367296 | bytes 647296 | tf_op jit(solution)/shard_map/while/body/eval_jaxpr/reduce_sum | solution.py:102
  274.7 7.7 %fusion.154 = (f32[32,32]{1,0:T(8,128)S(1)}, f32[32,32]{1,0:T(8,128)S(1)}) fusion(f32[32,384]{1,0:T(8,128)S(1)} %get-tuple-element.181, f32[32,384]{1,0:T(8,128)S(1)} %get-tuple-element.182, f32[32,384]{1,0:T(8,128)S(1)} %get-tuple-element.183, f32[32,384]{1,0:T(8,128)S(1)} %get-tuple-element.184, f32[32,384]{1,0:T(8,128)S(1)} %get-tuple-element.185, ...), kind=kLoop, calls=%fused_computation.13.clone.1 | loop fusion | flops 13367296 | bytes 647296 | tf_op jit(solution)/shard_map/while/body/eval_jaxpr/reduce_sum | solution.py:102
  283.4 7.7 %fusion.154 = (f32[32,32]{1,0:T(8,128)S(1)}, f32[32,32]{1,0:T(8,128)S(1)}) fusion(f32[32,384]{1,0:T(8,128)S(1)} %get-tuple-element.181, f32[32,384]{1,0:T(8,128)S(1)} %get-tuple-element.182, f32[32,384]{1,0:T(8,128)S(1)} %get-tuple-element.183, f32[32,384]{1,0:T(8,128)S(1)} %get-tuple-element.184, f32[32,384]{1,0:T(8,128)S(1)} %get-tuple-element.185, ...), kind=kLoop, calls=%fused_computation.13.clone.1 | loop fusion | flops 13367296 | bytes 647296 | tf_op jit(solution)/shard_map/while/body/eval_jaxpr/reduce_sum | solution.py:102
  292.2 7.7 %fusion.154 = (f32[32,32]{1,0:T(8,128)S(1)}, f32[32,32]{1,0:T(8,128)S(1)}) fusion(f32[32,384]{1,0:T(8,128)S(1)} %get-tuple-element.181, f32[32,384]{1,0:T(8,128)S(1)} %get-tuple-element.182, f32[32,384]{1,0:T(8,128)S(1)} %get-tuple-element.183, f32[32,384]{1,0:T(8,128)S(1)} %get-tuple-element.184, f32[32,384]{1,0:T(8,128)S(1)} %get-tuple-element.185, ...), kind=kLoop, calls=%fused_computation.13.clone.1 | loop fusion | flops 13367296 | bytes 647296 | tf_op jit(solution)/shard_map/while/body/eval_jaxpr/reduce_sum | solution.py:102
  301.0 7.7 %fusion.154 = (f32[32,32]{1,0:T(8,128)S(1)}, f32[32,32]{1,0:T(8,128)S(1)}) fusion(f32[32,384]{1,0:T(8,128)S(1)} %get-tuple-element.181, f32[32,384]{1,0:T(8,128)S(1)} %get-tuple-element.182, f32[32,384]{1,0:T(8,128)S(1)} %get-tuple-element.183, f32[32,384]{1,0:T(8,128)S(1)} %get-tuple-element.184, f32[32,384]{1,0:T(8,128)S(1)} %get-tuple-element.185, ...), kind=kLoop, calls=%fused_computation.13.clone.1 | loop fusion | flops 13367296 | bytes 647296 | tf_op jit(solution)/shard_map/while/body/eval_jaxpr/reduce_sum | solution.py:102
  309.7 7.7 %fusion.154 = (f32[32,32]{1,0:T(8,128)S(1)}, f32[32,32]{1,0:T(8,128)S(1)}) fusion(f32[32,384]{1,0:T(8,128)S(1)} %get-tuple-element.181, f32[32,384]{1,0:T(8,128)S(1)} %get-tuple-element.182, f32[32,384]{1,0:T(8,128)S(1)} %get-tuple-element.183, f32[32,384]{1,0:T(8,128)S(1)} %get-tuple-element.184, f32[32,384]{1,0:T(8,128)S(1)} %get-tuple-element.185, ...), kind=kLoop, calls=%fused_computation.13.clone.1 | loop fusion | flops 13367296 | bytes 647296 | tf_op jit(solution)/shard_map/while/body/eval_jaxpr/reduce_sum | solution.py:102
  318.5 7.7 %fusion.154 = (f32[32,32]{1,0:T(8,128)S(1)}, f32[32,32]{1,0:T(8,128)S(1)}) fusion(f32[32,384]{1,0:T(8,128)S(1)} %get-tuple-element.181, f32[32,384]{1,0:T(8,128)S(1)} %get-tuple-element.182, f32[32,384]{1,0:T(8,128)S(1)} %get-tuple-element.183, f32[32,384]{1,0:T(8,128)S(1)} %get-tuple-element.184, f32[32,384]{1,0:T(8,128)S(1)} %get-tuple-element.185, ...), kind=kLoop, calls=%fused_computation.13.clone.1 | loop fusion | flops 13367296 | bytes 647296 | tf_op jit(solution)/shard_map/while/body/eval_jaxpr/reduce_sum | solution.py:102
  327.2 7.7 %fusion.154 = (f32[32,32]{1,0:T(8,128)S(1)}, f32[32,32]{1,0:T(8,128)S(1)}) fusion(f32[32,384]{1,0:T(8,128)S(1)} %get-tuple-element.181, f32[32,384]{1,0:T(8,128)S(1)} %get-tuple-element.182, f32[32,384]{1,0:T(8,128)S(1)} %get-tuple-element.183, f32[32,384]{1,0:T(8,128)S(1)} %get-tuple-element.184, f32[32,384]{1,0:T(8,128)S(1)} %get-tuple-element.185, ...), kind=kLoop, calls=%fused_computation.13.clone.1 | loop fusion | flops 13367296 | bytes 647296 | tf_op jit(solution)/shard_map/while/body/eval_jaxpr/reduce_sum | solution.py:102
  335.8 11.8 %reduce-scatter.3.cloned.1.call-done = f32[128,1,64]{2,1,0:T(1,128)} async-done(((f32[256,1,64]{2,1,0:T(1,128)}), f32[128,1,64]{2,1,0:T(1,128)}) %reduce-scatter.3.cloned.1.call-update) | async-done | bytes 32784 | tf_op jit(solution)/shard_map/reduce_scatter | solution.py:40
  350.2 37.0 %reduce-scatter.5.cloned.1.call-done = f32[16,1,64]{2,1,0:T(1,128)} async-done(((f32[128,1,64]{2,1,0:T(1,128)}), f32[16,1,64]{2,1,0:T(1,128)}) %reduce-scatter.5.cloned.1.call-update) | async-done | bytes 4112 | tf_op jit(solution)/shard_map/reduce_scatter | solution.py:40
  387.2 10.7 %all-reduce = f32[16,1,64]{2,1,0:T(1,128)S(1)} all-reduce(f32[16,1,64]{2,1,0:T(1,128)} %reduce-scatter.5.cloned.1.call-done), channel_id=4, replica_groups=mesh['gx'=8,'gz_0'=4,'gz_1'=2,'row'=4] {'gz_0'}, use_global_device_ids=true, to_apply=%region_7.9.clone | all-reduce | flops 1024 | bytes 8192
  397.9 10.4 %all-reduce.1 = f32[4,1,64]{2,1,0:T(1,128)S(1)} all-reduce(f32[4,1,64]{2,1,0:T(1,128)S(1)} %constant_dynamic-slice_fusion.1), channel_id=5, replica_groups=mesh['gx'=8,'gz_0'=4,'gz_1'=2,'row'=4] {'row'}, use_global_device_ids=true, to_apply=%region_8.10.clone | all-reduce | flops 256 | bytes 2048
  (212 shorter events, 68.5 us)
Async XLA Ops:
  7.2 49.3 %copy-start = (f32[3,5,5]{2,0,1:T(4,128)S(1)}, f32[3,5,5]{2,0,1:T(4,128)}, u32[]{:S(2)}) copy-start(f32[3,5,5]{2,0,1:T(4,128)} %param.11) | copy-start | bytes 904
  7.2 15.2 %copy-start.1 = (f32[5,4,32,128]{3,2,1,0:T(8,128)S(1)}, f32[5,4,32,128]{3,2,1,0:T(8,128)}, u32[]{:S(2)}) copy-start(f32[5,4,32,128]{3,2,1,0:T(8,128)} %param.10) | copy-start | bytes 983044
  7.2 8.5 %copy-start.19 = (s32[6,64]{1,0:T(8,128)S(1)}, s32[6,64]{1,0:T(8,128)}, u32[]{:S(2)}) copy-start(s32[6,64]{1,0:T(8,128)} %param.13) | copy-start | bytes 4612
  7.2 340.4 %reduce-scatter.3.cloned.1.call-start = ((), (), s32[]{:S(2)}) async-start(), calls=%async_computation.2 | async-start | bytes 196608 | tf_op jit(solution)/shard_map/reduce_scatter | solution.py:40
  8.5 12.9 %collective-permute-start = (f32[5,3,32,128]{3,0,2,1:T(8,128)S(1)}, f32[5,3,32,128]{3,0,2,1:T(8,128)}, u32[]{:S(2)}, u32[]{:S(2)}) collective-permute-start(f32[5,3,32,128]{3,0,2,1:T(8,128)S(1)} %copy.276), channel_id=1, source_target_pairs={{0,32},{32,64},{64,96},{96,128},{128,160},{160,192},{192,224},{1,3... | collective-permute-start | bytes 737288 | tf_op jit(solution)/shard_map/ppermute | solution.py:28
  12.5 12.7 %collective-permute-start.1 = (f32[5,3,32,128]{3,0,2,1:T(8,128)S(1)}, f32[5,3,32,128]{3,0,2,1:T(8,128)S(1)}, u32[]{:S(2)}, u32[]{:S(2)}) collective-permute-start(f32[5,3,32,128]{3,0,2,1:T(8,128)S(1)} %copy.277), channel_id=1, source_target_pairs={{32,0},{64,32},{96,64},{128,96},{160,128},{192,160},{224,192},{33,... | collective-permute-start | bytes 737288 | tf_op jit(solution)/shard_map/ppermute | solution.py:29
  15.7 15.8 %copy-start.18 = (s32[384]{0:T(512)}, s32[384]{0:T(512)S(1)}, u32[]{:S(2)}) copy-start(s32[384]{0:T(512)S(1)} %reshape.434) | copy-start | bytes 4612
  25.2 3.2 collective-permute-start.2
  26.5 5.0 %collective-permute-start.3 = (f32[5,10,3,128]{3,0,2,1:T(8,128)S(1)}, f32[5,10,3,128]{3,0,2,1:T(8,128)S(1)}, u32[]{:S(2)}, u32[]{:S(2)}) collective-permute-start(f32[5,10,3,128]{3,0,2,1:T(8,128)S(1)} %get-tuple-element.114), channel_id=1, source_target_pairs={{4,0},{8,4},{12,8},{16,12},{20,16},{24,20},{28,24},{5,1},{9,5},{13... | collective-permute-start | bytes 230408 | tf_op jit(solution)/shard_map/ppermute | solution.py:29
  28.4 3.1 copy-start.11
  31.6 0.6 copy-start.12
  35.9 7.9 %collective-permute-start.4 = (f32[5,10,38,3]{2,3,1,0:T(4,128)S(1)}, f32[5,10,38,3]{2,3,1,0:T(4,128)}, u32[]{:S(2)}, u32[]{:S(2)}) collective-permute-start(f32[5,10,38,3]{2,3,1,0:T(4,128)S(1)} %copy.132), channel_id=1, source_target_pairs={{0,1},{1,2},{2,3},{4,5},{5,6},{6,7},{8,9},{9,10},{10,11},{12,13},{... | collective-permute-start | bytes 68408 | tf_op jit(solution)/shard_map/ppermute | solution.py:28
  41.1 6.9 %collective-permute-start.5 = (f32[5,10,38,3]{2,3,1,0:T(4,128)}, f32[5,10,38,3]{2,3,1,0:T(4,128)}, u32[]{:S(2)}, u32[]{:S(2)}) collective-permute-start(f32[5,10,38,3]{2,3,1,0:T(4,128)} %copy.133), channel_id=1, source_target_pairs={{1,0},{2,1},{3,2},{5,4},{6,5},{7,6},{9,8},{10,9},{11,10},{13,12},{... | collective-permute-start | bytes 68408 | tf_op jit(solution)/shard_map/ppermute | solution.py:29
  53.4 3.1 copy-start.4
  76.1 8.0 %copy-start.23 = (f32[3,256]{1,0:T(4,128)S(1)}, f32[3,256]{1,0:T(4,128)}, u32[]{:S(2)}) copy-start(f32[3,256]{1,0:T(4,128)} %param.15) | copy-start | bytes 9220
  76.1 8.0 %copy-start.20 = (s32[6,64]{1,0:T(8,128)S(1)}, s32[6,64]{1,0:T(8,128)}, u32[]{:S(2)}) copy-start(s32[6,64]{1,0:T(8,128)} %param.13) | copy-start | bytes 4612
  77.1 13.5 %collective-permute-start.6 = (f32[5,3,32,128]{3,0,2,1:T(8,128)S(1)}, f32[5,3,32,128]{3,0,2,1:T(8,128)S(1)}, u32[]{:S(2)}, u32[]{:S(2)}) collective-permute-start(f32[5,3,32,128]{3,0,2,1:T(8,128)S(1)} %get-tuple-element.117), channel_id=1, source_target_pairs={{0,32},{32,64},{64,96},{96,128},{128,160},{160,192},{192,224},{1,3... | collective-permute-start | bytes 737288 | tf_op jit(solution)/shard_map/ppermute | solution.py:28
  82.2 13.7 %collective-permute-start.7 = (f32[5,3,32,128]{3,0,2,1:T(8,128)S(1)}, f32[5,3,32,128]{3,0,2,1:T(8,128)S(1)}, u32[]{:S(2)}, u32[]{:S(2)}) collective-permute-start(f32[5,3,32,128]{3,0,2,1:T(8,128)S(1)} %get-tuple-element.118), channel_id=1, source_target_pairs={{32,0},{64,32},{96,64},{128,96},{160,128},{192,160},{224,192},{33,... | collective-permute-start | bytes 737288 | tf_op jit(solution)/shard_map/ppermute | solution.py:29
  95.9 4.9 %collective-permute-start.8 = (f32[5,10,3,128]{3,0,2,1:T(8,128)S(1)}, f32[5,10,3,128]{3,0,2,1:T(8,128)S(1)}, u32[]{:S(2)}, u32[]{:S(2)}) collective-permute-start(f32[5,10,3,128]{3,0,2,1:T(8,128)S(1)} %get-tuple-element.111), channel_id=1, source_target_pairs={{0,4},{4,8},{8,12},{12,16},{16,20},{20,24},{24,28},{1,5},{5,9},{9,... | collective-permute-start | bytes 230408 | tf_op jit(solution)/shard_map/ppermute | solution.py:28
  98.7 6.2 %collective-permute-start.9 = (f32[5,10,3,128]{3,0,2,1:T(8,128)S(1)}, f32[5,10,3,128]{3,0,2,1:T(8,128)S(1)}, u32[]{:S(2)}, u32[]{:S(2)}) collective-permute-start(f32[5,10,3,128]{3,0,2,1:T(8,128)S(1)} %get-tuple-element.112), channel_id=1, source_target_pairs={{4,0},{8,4},{12,8},{16,12},{20,16},{24,20},{28,24},{5,1},{9,5},{13... | collective-permute-start | bytes 230408 | tf_op jit(solution)/shard_map/ppermute | solution.py:29
  108.6 6.4 %collective-permute-start.10 = (f32[5,10,38,3]{2,3,1,0:T(4,128)S(1)}, f32[5,10,38,3]{2,3,1,0:T(4,128)}, u32[]{:S(2)}, u32[]{:S(2)}) collective-permute-start(f32[5,10,38,3]{2,3,1,0:T(4,128)S(1)} %copy.145), channel_id=1, source_target_pairs={{0,1},{1,2},{2,3},{4,5},{5,6},{6,7},{8,9},{9,10},{10,11},{12,13},{... | collective-permute-start | bytes 68408 | tf_op jit(solution)/shard_map/ppermute | solution.py:28
  113.2 6.9 %collective-permute-start.11 = (f32[5,10,38,3]{2,3,1,0:T(4,128)}, f32[5,10,38,3]{2,3,1,0:T(4,128)}, u32[]{:S(2)}, u32[]{:S(2)}) collective-permute-start(f32[5,10,38,3]{2,3,1,0:T(4,128)} %copy.146), channel_id=1, source_target_pairs={{1,0},{2,1},{3,2},{5,4},{6,5},{7,6},{9,8},{10,9},{11,10},{13,12},{... | collective-permute-start | bytes 68408 | tf_op jit(solution)/shard_map/ppermute | solution.py:29
  128.5 5.4 %copy-start.5 = (f32[8,36,132]{2,1,0:T(8,128)S(1)}, f32[8,36,132]{2,1,0:T(8,128)}, u32[]{:S(2)}) copy-start(f32[8,36,132]{2,1,0:T(8,128)} %and_convert_fusion) | copy-start | bytes 456196
  150.4 20.7 %copy-start.21 = (s32[384]{0:T(512)S(1)}, s32[384]{0:T(512)}, u32[]{:S(2)}) copy-start(s32[384]{0:T(512)} %compare_select_fusion.2) | copy-start | bytes 4612
  150.4 12.8 %collective-permute-start.12 = (f32[5,3,32,128]{3,0,2,1:T(8,128)S(1)}, f32[5,3,32,128]{3,0,2,1:T(8,128)S(1)}, u32[]{:S(2)}, u32[]{:S(2)}) collective-permute-start(f32[5,3,32,128]{3,0,2,1:T(8,128)S(1)} %get-tuple-element.115), channel_id=1, source_target_pairs={{0,32},{32,64},{64,96},{96,128},{128,160},{160,192},{192,224},{1,3... | collective-permute-start | bytes 737288 | tf_op jit(solution)/shard_map/ppermute | solution.py:28
  154.1 13.1 %collective-permute-start.13 = (f32[5,3,32,128]{3,0,2,1:T(8,128)S(1)}, f32[5,3,32,128]{3,0,2,1:T(8,128)S(1)}, u32[]{:S(2)}, u32[]{:S(2)}) collective-permute-start(f32[5,3,32,128]{3,0,2,1:T(8,128)S(1)} %get-tuple-element.116), channel_id=1, source_target_pairs={{32,0},{64,32},{96,64},{128,96},{160,128},{192,160},{224,192},{33,... | collective-permute-start | bytes 737288 | tf_op jit(solution)/shard_map/ppermute | solution.py:29
  167.2 8.5 %copy-start.2 = (f32[5,3,32,128]{3,0,2,1:T(8,128)}, f32[5,3,32,128]{3,0,2,1:T(8,128)S(1)}, u32[]{:S(2)}) copy-start(f32[5,3,32,128]{3,0,2,1:T(8,128)S(1)} %collective-permute-done.13) | copy-start | bytes 737284
  167.2 3.8 collective-permute-start.14
  169.7 5.9 %collective-permute-start.15 = (f32[5,10,3,128]{3,0,2,1:T(8,128)S(1)}, f32[5,10,3,128]{3,0,2,1:T(8,128)S(1)}, u32[]{:S(2)}, u32[]{:S(2)}) collective-permute-start(f32[5,10,3,128]{3,0,2,1:T(8,128)S(1)} %get-tuple-element.110), channel_id=1, source_target_pairs={{4,0},{8,4},{12,8},{16,12},{20,16},{24,20},{28,24},{5,1},{9,5},{13... | collective-permute-start | bytes 230408 | tf_op jit(solution)/shard_map/ppermute | solution.py:29
  175.7 0.6 copy-start.9
  180.0 26.7 %collective-permute-start.16 = (f32[5,10,38,3]{2,3,1,0:T(4,128)S(1)}, f32[5,10,38,3]{2,3,1,0:T(4,128)}, u32[]{:S(2)}, u32[]{:S(2)}) collective-permute-start(f32[5,10,38,3]{2,3,1,0:T(4,128)S(1)} %copy.158), channel_id=1, source_target_pairs={{0,1},{1,2},{2,3},{4,5},{5,6},{6,7},{8,9},{9,10},{10,11},{12,13},{... | collective-permute-start | bytes 68408 | tf_op jit(solution)/shard_map/ppermute | solution.py:28
  184.3 24.0 %collective-permute-start.17 = (f32[5,10,38,3]{2,3,1,0:T(4,128)}, f32[5,10,38,3]{2,3,1,0:T(4,128)}, u32[]{:S(2)}, u32[]{:S(2)}) collective-permute-start(f32[5,10,38,3]{2,3,1,0:T(4,128)} %copy.159), channel_id=1, source_target_pairs={{1,0},{2,1},{3,2},{5,4},{6,5},{7,6},{9,8},{10,9},{11,10},{13,12},{... | collective-permute-start | bytes 68408 | tf_op jit(solution)/shard_map/ppermute | solution.py:29
  206.6 4.4 %copy-start.3 = (f32[5,3,32,128]{3,0,2,1:T(8,128)S(1)}, f32[5,3,32,128]{3,0,2,1:T(8,128)}, u32[]{:S(2)}) copy-start(f32[5,3,32,128]{3,0,2,1:T(8,128)} %copy-done.2) | copy-start | bytes 737284
  206.6 4.4 %copy-start.10 = (f32[5,10,3,128]{3,0,2,1:T(8,128)S(1)}, f32[5,10,3,128]{3,0,2,1:T(8,128)}, u32[]{:S(2)}) copy-start(f32[5,10,3,128]{3,0,2,1:T(8,128)} %copy-done.9) | copy-start | bytes 230404
  218.2 7.3 %copy-start.6 = (f32[8,36,132]{2,1,0:T(8,128)S(1)}, f32[8,36,132]{2,1,0:T(8,128)}, u32[]{:S(2)}) copy-start(f32[8,36,132]{2,1,0:T(8,128)} %and_convert_fusion) | copy-start | bytes 456196
  241.8 10.1 %copy-start.13 = (f32[384,5]{1,0:T(8,128)S(1)}, f32[384,5]{1,0:T(8,128)}, u32[]{:S(2)}) copy-start(f32[384,5]{1,0:T(8,128)} %gather_fusion) | copy-start | bytes 23044
  241.8 10.1 %copy-start.14 = (f32[384,5]{1,0:T(8,128)S(1)}, f32[384,5]{1,0:T(8,128)}, u32[]{:S(2)}) copy-start(f32[384,5]{1,0:T(8,128)} %gather_fusion.1) | copy-start | bytes 23044
  241.8 10.1 %copy-start.24 = (pred[384]{0:T(512)(128)(4,1)S(1)}, pred[384]{0:T(512)(128)(4,1)}, u32[]{:S(2)}) copy-start(pred[384]{0:T(512)(128)(4,1)} %compare_and_fusion) | copy-start | bytes 1156
  262.4 1.2 copy-start.7
  262.4 1.2 copy-start.16
  262.4 1.2 copy-start.17
  262.4 1.2 copy-start.22
  263.6 1.4 copy-start.8
  263.6 1.4 copy-start.15
  265.0 82.6 %copy-start.26 = (u32[256]{0:T(256)S(1)}, u32[256]{0:T(256)}, u32[]{:S(2)}) copy-start(u32[256]{0:T(256)} %constant.201) | copy-start | bytes 3076
  265.0 83.2 %copy-start.25 = (u32[256]{0:T(256)S(1)}, u32[256]{0:T(256)}, u32[]{:S(2)}) copy-start(u32[256]{0:T(256)} %constant.205) | copy-start | bytes 3076
  335.7 51.5 %reduce-scatter.5.cloned.1.call-start = ((), (), s32[]{:S(2)}) async-start(), calls=%async_computation.3 | async-start | bytes 73728 | tf_op jit(solution)/shard_map/reduce_scatter | solution.py:40
Sparse Core Ops, SparseCore 0:
  335.8 11.6 reduce-scatter.2
  350.1 37.0 reduce-scatter.4
where the time goes:
time: 421 us; the launch traced here: 417 us
  other arithmetic  120 us (29%)
  waiting for transfers between devices  94.7 us (22%)
  local copies, waits for them, and re-layouts  81.8 us (19%)
  starting transfers between devices  44.9 us (11%)
  matrix products  37.3 us (9%)
  blocking collectives  21.1 us (5%)
  between operations  16.6 us (4%)
    reduce_sum x8, other arithmetic, radiate(): jnp.sum(plus_weight * dip_real - minus_weight * dip_imag + sine * mono_re...  61.9 us
    reduce_scatter x2, waiting for transfers between devices, reduced_to_own(): tiles = lax.psum_scatter(tiles, axes[k], scatter_dimension=0, tiled=True)  48.8 us
    dot_general x9, matrix products, stencil_rate(): jnp.einsum('dvw,dwxzr->vxzr', flux_jacobian, slopes, precision=lax.Precis...  35.9 us
    ppermute x9, starting transfers between devices, padded_2(): before = lax.ppermute(last, axis, up)  29.6 us
    ppermute x9, waiting for transfers between devices, padded_2(): after = lax.ppermute(leading, axis, down)  29.6 us
    unnamed x2, blocking collectives  21.1 us
    another operation x9, other arithmetic, stencil_rate(): slopes = jnp.stack([along_x, along_z, along_r])  19.6 us
    ppermute x9, waiting for transfers between devices, padded_2(): before = lax.ppermute(last, axis, up)  16.3 us
  transfers between devices with their start and end apart: 20, of which 13 were waited for; matrix products, arithmetic and copies ran while one was open for 9% of the time, Pallas kernels for 0%

commit v1 on v0

v1 whole, which is shorter than its diff:
```python
import functools
import math

import jax
import jax.numpy as jnp
import numpy as np
from jax import lax
from jax.experimental import pallas as pl
from jax.experimental.pallas import tpu as pltpu
from jax.sharding import PartitionSpec as P

F32 = jnp.float32
MESH = pl.DeviceIdType.MESH
NV = 5
FREQ = 32
STEPS = 3
SURF_DEV = 128
TIME_STEP = 0.3
VISCOSITY = 0.05
PAD = 8
STAGES = ((0.0, 1.0), (0.75, 0.25), (1.0 / 3.0, 2.0 / 3.0))
AXES = ("gx", "gz", "row")


def split_dot(left, right):
    total = None
    for _ in range(3):
        part = left.astype(jnp.bfloat16)
        left = left - part.astype(F32)
        piece = jnp.dot(part, right, preferred_element_type=F32)
        total = piece if total is None else total + piece
    return total


def stencil_kernel(
    sizes, jac, cells, flow, field, samples,
    U, xr, zs, zr, rs, rr, load_sem, send_sem, recv_sem,
):
    nx, nz, nr, cx, cz, cr = sizes
    slots = cells.shape[1]
    index = [lax.axis_index(a) for a in AXES]
    counts = (nx, nz, nr)

    there = []
    for axis in range(3):
        there.append((index[axis] > 0, index[axis] < counts[axis] - 1))

    def peer(axis, side):
        ids = list(index)
        ids[axis] = index[axis] + (1 if side else -1)
        return tuple(ids)

    load = pltpu.make_async_copy(flow, U.at[0, :, :, pl.ds(PAD, cz), :], load_sem.at[0])
    load.start()

    barrier = pltpu.get_barrier_semaphore()
    for axis in range(3):
        for side in range(2):
            @pl.when(there[axis][side])
            def _():
                pl.semaphore_signal(barrier, inc=1, device_id=peer(axis, side), device_id_type=MESH)
    peers = sum(flag.astype(jnp.int32) for pair in there for flag in pair)
    pl.semaphore_wait(barrier, peers)

    for slot in range(3):
        for axis, buffer in enumerate((xr, zr, rr)):
            for side in range(2):
                @pl.when(jnp.logical_not(there[axis][side]))
                def _():
                    view = buffer.at[slot, side]
                    view[...] = jnp.zeros(view.shape, F32)
    load.wait()

    lane = lax.broadcasted_iota(jnp.int32, (cz, cr), 1)

    def copy(axis, side, slot):
        if axis == 0:
            src = U.at[slot, :, (cx - 1) if side else 0, pl.ds(PAD, cz), :]
            dst = xr.at[slot, 1 - side]
        elif axis == 1:
            src = zs.at[slot, side]
            dst = zr.at[slot, 1 - side]
        else:
            src = rs.at[slot]
            dst = rr.at[slot, 1 - side]
        return pltpu.make_async_remote_copy(
            src_ref=src, dst_ref=dst,
            send_sem=send_sem.at[axis, side, slot],
            recv_sem=recv_sem.at[axis, 1 - side, slot],
            device_id=peer(axis, side), device_id_type=MESH,
        )

    def incoming(axis, side, slot):
        if axis == 0:
            src = U.at[slot, :, 0, pl.ds(PAD, cz), :]
            dst = xr.at[slot, side]
        elif axis == 1:
            src = zs.at[slot, side]
            dst = zr.at[slot, side]
        else:
            src = rs.at[slot]
            dst = rr.at[slot, side]
        return pltpu.make_async_remote_copy(
            src_ref=src, dst_ref=dst,
            send_sem=send_sem.at[axis, side, slot],
            recv_sem=recv_sem.at[axis, side, slot],
            device_id=peer(axis, side), device_id_type=MESH,
        )

    def for_sides(axis, act):
        for side in range(2):
            @pl.when(there[axis][side])
            def _():
                act(axis, side)

    def start_x(slot):
        for_sides(0, lambda axis, side: copy(axis, side, slot).start())

    def start_zr(slot):
        packed = jnp.zeros((cz, cr), F32)
        for v in range(NV):
            for x in range(cx):
                k = 2 * (v * cx + x)
                value = U[slot, v, x, PAD:PAD + cz, :]
                zs[slot, 0, v, x:x + 1, :] = value[:1]
                zs[slot, 1, v, x:x + 1, :] = value[cz - 1:]
                turned = pltpu.roll(value, k, 1) if k else value
                packed = jnp.where((lane == k) | (lane == (k - 1) % cr), turned, packed)
        rs[slot] = packed
        for axis in (1, 2):
            for_sides(axis, lambda axis, side: copy(axis, side, slot).start())

    def wait_sent(slot):
        for axis in range(3):
            for_sides(axis, lambda axis, side: copy(axis, side, slot).wait_send())

    def wait_received(slot):
        for axis in range(3):
            for_sides(axis, lambda axis, side: incoming(axis, side, slot).wait_recv())

    def stage(j, send):
        src, dst = j, (j + 1) % 3
        keep, gain = STAGES[j]
        wait_received(src)
        for v in range(NV):
            for x in range(cx):
                U[src, v, x, PAD - 1:PAD, :] = zr[src, 0, v, x:x + 1, :]
                U[src, v, x, PAD + cz:PAD + cz + 1, :] = zr[src, 1, v, x:x + 1, :]
        halo = jnp.where(lane % 2 == 1, rr[src, 0], rr[src, 1])

        def layer(x):
            sums = [None] * NV
            rest = []
            for w in range(NV):
                center = U[src, w, x, PAD:PAD + cz, :]
                below = xr[src, 0, w] if x == 0 else U[src, w, x - 1, PAD:PAD + cz, :]
                above = xr[src, 1, w] if x == cx - 1 else U[src, w, x + 1, PAD:PAD + cz, :]
                before = U[src, w, x, PAD - 1:PAD + cz - 1, :]
                after = U[src, w, x, PAD + 1:PAD + cz + 1, :]
                k = 2 * (w * cx + x)
                turned = pltpu.roll(halo, cr - k, 1) if k else halo
                inner = pltpu.roll(jnp.where(lane == cr - 1, turned, center), 1, 1)
                outer = pltpu.roll(jnp.where(lane == 0, turned, center), cr - 1, 1)
                slopes = (above - below, after - before, outer - inner)
                beside = above + below + after + before + outer + inner
                rest.append(
                    beside * (gain * TIME_STEP * VISCOSITY)
                    + center * (gain * (1.0 - 6.0 * VISCOSITY * TIME_STEP))
                )
                for v in range(NV):
                    for d in range(3):
                        piece = slopes[d] * jac[(d * NV + v) * NV + w]
                        sums[v] = piece if sums[v] is None else sums[v] + piece
            for v in range(NV):
                value = sums[v] * (0.5 * gain * TIME_STEP) + rest[v]
                if keep:
                    value = value + U[0, v, x, PAD:PAD + cz, :] * keep
                U[dst, v, x, PAD:PAD + cz, :] = value

        layer(0)
        layer(cx - 1)
        if send is True:
            start_x(dst)
        else:
            pl.when(send)(lambda: start_x(dst))
        for x in range(1, cx - 1):
            layer(x)
        wait_sent(src)
        if send is True:
            start_zr(dst)
        else:
            pl.when(send)(lambda: start_zr(dst))

    spot = cells[...]
    spot_lane = spot % cr
    spot_row = spot // cr
    height = lax.broadcasted_iota(jnp.int32, (cr, slots), 0)
    rows = lax.broadcasted_iota(jnp.int32, (cx * cz, slots), 0)

    def sample(step):
        chosen_lane = jnp.where(height == spot_lane, 1.0, 0.0).astype(jnp.bfloat16)
        for j in range(4):
            tile = jnp.concatenate([U[0, j, x, PAD:PAD + cz, :] for x in range(cx)], axis=0)
            if j == 0:
                tile = tile + jnp.concatenate([U[0, 4, x, PAD:PAD + cz, :] for x in range(cx)], axis=0)
            picked = split_dot(tile, chosen_lane)
            picked = jnp.where(rows == spot_row, picked, 0.0)
            samples[pl.ds(step, 1), j:j + 1, :] = jnp.sum(picked, axis=0, keepdims=True)[None]

    start_x(0)
    start_zr(0)

    def step_body(step, carry):
        stage(0, True)
        stage(1, True)
        stage(2, step < STEPS - 1)
        sample(step)
        return carry

    lax.fori_loop(0, STEPS, step_body, 0)
    out = pltpu.make_async_copy(U.at[0, :, :, pl.ds(PAD, cz), :], field, load_sem.at[1])
    out.start()
    out.wait()


def run_stencil(sizes, jac, cells, flow):
    cx, cz, cr = sizes[3:]
    slots = cells.shape[1]
    return pl.pallas_call(
        functools.partial(stencil_kernel, sizes),
        out_shape=(
            jax.ShapeDtypeStruct(flow.shape, F32),
            jax.ShapeDtypeStruct((STEPS, 8, slots), F32),
        ),
        in_specs=[
            pl.BlockSpec(memory_space=pltpu.SMEM),
            pl.BlockSpec(memory_space=pltpu.VMEM),
            pl.BlockSpec(memory_space=pl.ANY),
        ],
        out_specs=(
            pl.BlockSpec(memory_space=pl.ANY),
            pl.BlockSpec(memory_space=pltpu.VMEM),
        ),
        scratch_shapes=[
            pltpu.VMEM((3, NV, cx, cz + 2 * PAD, cr), F32),
            pltpu.VMEM((3, 2, NV, cz, cr), F32),
            pltpu.VMEM((3, 2, NV, cx, cr), F32),
            pltpu.VMEM((3, 2, NV, cx, cr), F32),
            pltpu.VMEM((3, cz, cr), F32),
            pltpu.VMEM((3, 2, cz, cr), F32),
            pltpu.SemaphoreType.DMA((2,)),
            pltpu.SemaphoreType.DMA((3, 2, 3)),
            pltpu.SemaphoreType.DMA((3, 2, 3)),
        ],
        compiler_params=pltpu.CompilerParams(
            collective_id=0, has_side_effects=True, vmem_limit_bytes=40 << 20
        ),
        name="stencil",
    )(jac, cells, flow)


def poly(x, coefficients):
    total = jnp.full_like(x, coefficients[-1])
    for c in coefficients[-2::-1]:
        total = total * x + c
    return total


SIN = [(-1.0) ** n / math.factorial(2 * n + 1) for n in range(9)]
COS = [(-1.0) ** n / math.factorial(2 * n) for n in range(10)]


def radiate_kernel(sizes, table, cells, blocks, watch, history, samples, out, held, spec, place, seat, sem):
    nx, nz, nr, cx, cz, cr = sizes
    slots = cells.shape[1]
    times = history.shape[2]
    grid = (nx * cx, nz * cz, nr * cr)
    groups = slots // 128
    observers = watch.shape[0]
    copies = [
        pltpu.make_async_copy(history.at[:, v, :], held.at[v], sem.at[v]) for v in range(NV)
    ]
    for c in copies:
        c.start()
    spot = cells[...]
    index = [lax.axis_index(a) for a in AXES]
    place[0:1, :] = (index[0] * cx + spot // (cz * cr)).astype(F32) + 0.5
    place[1:2, :] = (index[1] * cz + spot // cr % cz).astype(F32) + 0.5
    place[2:3, :] = (index[2] * cr + spot % cr).astype(F32) + 0.5
    for c in copies:
        c.wait()
    fourier = table[...]
    time = lax.broadcasted_iota(jnp.int32, fourier.shape, 1)
    early = jnp.where(time < times - STEPS, fourier, 0.0)
    for j in range(4):
        signal = held[j] + held[4] if j == 0 else held[j]
        spectrum = lax.dot_general(
            early, signal, (((1,), (1,)), ((), ())),
            precision=lax.Precision.HIGHEST, preferred_element_type=F32,
        )
        for t in range(STEPS):
            column = fourier[:, times - STEPS + t:times - STEPS + t + 1]
            spectrum = spectrum + column * samples[t, j:j + 1, :]
        spec[j] = spectrum
    live = lax.broadcasted_iota(jnp.int32, (8, 128), 1)
    live_count = blocks[0] * 64
    unit = 2.0 / grid[2]
    middle = 2.3
    lane = lax.broadcasted_iota(jnp.int32, (8, 128), 1)
    norm = 1.0 / math.sqrt(nx * nz * nr * SURF_DEV)

    def tile(i, carry):
        rows = pl.ds(pl.multiple_of(i * 8, 8), 8)
        seats = watch[rows, :]
        at = (
            seats[:, 0:1] * float(grid[0]),
            seats[:, 1:2] * float(grid[1]),
            (1.25 + 0.75 * seats[:, 2:3]) * float(grid[2]),
        )
        state = []
        for g in range(groups):
            cols = slice(g * 128, (g + 1) * 128)
            away = [at[d] - place[d:d + 1, cols] for d in range(3)]
            square = away[0] * away[0] + away[1] * away[1] + away[2] * away[2]
            distance = jnp.sqrt(square)
            inverse = 1.0 / distance
            unit_vec = [w * inverse for w in away]
            angle = distance * unit - middle
            sq = angle * angle
            sine = angle * poly(sq, SIN)
            cosine = poly(sq, COS)
            cm, sm = math.cos(middle), math.sin(middle)
            zr = cosine * cm - sine * sm
            zi = -(sine * cm + cosine * sm)
            amp = jnp.where(live + g * 128 < live_count, inverse * (grid[2] * norm), 0.0)
            near = inverse * (1.0 / unit)
            state.append([unit_vec, near, zr, zi, amp * zr, amp * zi])
        result = jnp.zeros((8, 128), F32)
        for f in range(FREQ):
            real, imag = None, None
            for g in range(groups):
                cols = slice(g * 128, (g + 1) * 128)
                unit_vec, near, zr, zi, ur, ui = state[g]
                sr = [spec[j, f:f + 1, cols] for j in range(4)]
                si = [spec[j, FREQ + f:FREQ + f + 1, cols] for j in range(4)]
                dr = unit_vec[0] * sr[1] + unit_vec[1] * sr[2] + unit_vec[2] * sr[3]
                di = unit_vec[0] * si[1] + unit_vec[1] * si[2] + unit_vec[2] * si[3]
                w = near * (1.0 / (f + 1))
                gr = w * dr - (si[0] + di)
                gi = w * di + (sr[0] + dr)
                pr = ur * gr - ui * gi
                pi = ur * gi + ui * gr
                real = pr if real is None else real + pr
                imag = pi if imag is None else imag + pi
                if f < FREQ - 1:
                    state[g][4] = ur * zr - ui * zi
                    state[g][5] = ur * zi + ui * zr
            result = jnp.where(lane == f, jnp.sum(real, axis=1, keepdims=True), result)
            result = jnp.where(lane == FREQ + f, jnp.sum(imag, axis=1, keepdims=True), result)
        out[rows, :] = result
        return carry

    lax.fori_loop(0, observers // 8, tile, 0)


def run_radiate(sizes, table, cells, blocks, watch, history, samples):
    slots = cells.shape[1]
    vm = pl.BlockSpec(memory_space=pltpu.VMEM)
    return pl.pallas_call(
        functools.partial(radiate_kernel, sizes),
        out_shape=jax.ShapeDtypeStruct((watch.shape[0], 128), F32),
        in_specs=[vm, vm, pl.BlockSpec(memory_space=pltpu.SMEM), vm, pl.BlockSpec(memory_space=pl.ANY), vm],
        out_specs=vm,
        scratch_shapes=[
            pltpu.VMEM((NV, slots, history.shape[2]), F32),
            pltpu.VMEM((4, 2 * FREQ, slots), F32),
            pltpu.VMEM((8, slots), F32),
            pltpu.VMEM((8, 128), F32),
            pltpu.SemaphoreType.DMA((NV,)),
        ],
        compiler_params=pltpu.CompilerParams(vmem_limit_bytes=40 << 20),
        name="radiate",
    )(table, cells, blocks, watch, history, samples)


def reduce_kernel(counts, value, out, got, rows, last, send1, recv1, send2, recv2):
    nx, nz, nr = counts
    plane = nz * nr
    a, b, c = [lax.axis_index(x) for x in AXES]
    place = b * nr + c

    def along(d):
        return (lax.rem(a + d, nx), b, c)

    def across(d):
        other = lax.rem(place + d, plane)
        return (a, other // nr, lax.rem(other, nr))

    barrier = pltpu.get_barrier_semaphore()
    for d in range(1, nx):
        pl.semaphore_signal(barrier, inc=1, device_id=along(d), device_id_type=MESH)
    for d in range(1, plane):
        pl.semaphore_signal(barrier, inc=1, device_id=across(d), device_id_type=MESH)
    pl.semaphore_wait(barrier, nx - 1 + plane - 1)

    first = []
    for d in range(1, nx):
        to = lax.rem(a + d, nx)
        first.append(pltpu.make_async_remote_copy(
            src_ref=value.at[pl.ds(pl.multiple_of(to * plane, plane), plane)],
            dst_ref=got.at[d - 1], send_sem=send1.at[d - 1], recv_sem=recv1.at[d - 1],
            device_id=along(d), device_id_type=MESH,
        ))
    for x in first:
        x.start()
    total = value[pl.ds(pl.multiple_of(a * plane, plane), plane)]
    for d in range(1, nx):
        first[d - 1].wait_recv()
        total = total + got[d - 1]
    rows[...] = total[:, None, :]
    second = []
    for d in range(1, plane):
        to = lax.rem(place + d, plane)
        second.append(pltpu.make_async_remote_copy(
            src_ref=rows.at[to], dst_ref=last.at[d - 1],
            send_sem=send2.at[d - 1], recv_sem=recv2.at[d - 1],
            device_id=across(d), device_id_type=MESH,
        ))
    for x in second:
        x.start()
    for x in second:
        x.wait_recv()
    total = rows[place] + jnp.sum(last[...], axis=0)
    out[...] = total[:, :out.shape[1]]
    for x in first + second:
        x.wait_send()


def run_reduce(counts, value):
    nx, nz, nr = counts
    plane = nz * nr
    return pl.pallas_call(
        functools.partial(reduce_kernel, counts),
        out_shape=jax.ShapeDtypeStruct((1, 2 * FREQ), F32),
        in_specs=[pl.BlockSpec(memory_space=pltpu.VMEM)],
        out_specs=pl.BlockSpec(memory_space=pltpu.VMEM),
        scratch_shapes=[
            pltpu.VMEM((nx - 1, plane, 128), F32),
            pltpu.VMEM((plane, 1, 128), F32),
            pltpu.VMEM((plane - 1, 1, 128), F32),
            pltpu.SemaphoreType.DMA((nx - 1,)),
            pltpu.SemaphoreType.DMA((nx - 1,)),
            pltpu.SemaphoreType.DMA((plane - 1,)),
            pltpu.SemaphoreType.DMA((plane - 1,)),
        ],
        compiler_params=pltpu.CompilerParams(
            collective_id=1, has_side_effects=True, vmem_limit_bytes=40 << 20
        ),
        name="reduce",
    )(value)


def fourier_table(samples):
    turns = np.arange(1, FREQ + 1)[:, None] * np.arange(samples)[None, :] % samples
    angles = 2.0 * np.pi * turns / samples
    return (np.concatenate([np.cos(angles), -np.sin(angles)]) / np.sqrt(samples)).astype(np.float32)


def solution(mesh):
    counts = tuple(mesh.shape[a] for a in AXES)

    def per_device(flow, jacobian, history, cell, blocks, observers):
        sizes = counts + flow.shape[1:]
        cells = cell.reshape(1, -1)
        field, samples = run_stencil(sizes, jacobian.reshape(-1), cells, flow)
        table = jnp.asarray(fourier_table(history.shape[2]))
        value = run_radiate(sizes, table, cells, blocks.reshape(-1), observers.T, history, samples)
        return field, run_reduce(counts, value)

    return jax.shard_map(
        per_device,
        mesh=mesh,
        in_specs=(
            P(None, "gx", "gz", "row"),
            P(),
            P(AXES, None, None),
            P(AXES, None),
            P("row", ("gx", "gz")),
            P(),
        ),
        out_specs=(P(None, "gx", "gz", "row"), P(AXES, None)),
        check_vma=False,
    )
```

time: 421 us -> 93 us (0.22)
  the two profiles are of different devices: /device:TPU:32 before, /device:TPU:1 now
where the time goes in v1:
time: 93 us; the launch traced here: 92.7 us
  Pallas kernels  85 us (91%)
  local copies, waits for them, and re-layouts  6.4 us (7%)
  between operations  1.34 us (1%)
    pallas_call x1, Pallas kernels, run_stencil(): pl.pallas_call(functools.partial(stencil_kernel, sizes), out_shape=(jax.S...  46.5 us
    pallas_call x1, Pallas kernels, run_radiate(): pl.pallas_call(functools.partial(radiate_kernel, sizes), out_shape=jax.Sh...  20.1 us
    pallas_call x1, Pallas kernels, run_reduce(): pl.pallas_call(functools.partial(reduce_kernel, counts), out_shape=jax.Sh...  18.4 us
    unnamed x9, local copies, waits for them, and re-layouts  5.55 us

profile of v1, /device:TPU:1, one launch (start us, length us, event | category | flops | bytes accessed | tf_op | source)
XLA Modules:
  0.0 92.7 jit_solution(7654887557961957111)
XLA Ops:
  0.6 0.0 copy-start.1
  1.3 0.8 reshape.14.cells
  2.1 0.7 copy.12
  2.8 0.1 reshape.13.jac
  2.8 0.8 copy.13
  3.7 0.0 copy-start
  3.7 1.0 %copy-done = f32[5,4,32,128]{3,2,1,0:T(8,128)S(1)} copy-done((f32[5,4,32,128]{3,2,1,0:T(8,128)S(1)}, f32[5,4,32,128]{3,2,1,0:T(8,128)}, u32[]{:S(2)}) %copy-start) | copy-done | bytes 327704
  4.7 46.5 %stencil.1 = (f32[5,4,32,128]{3,2,1,0:T(8,128)S(1)}, f32[3,8,384]{2,1,0:T(8,128)S(1)}) custom-call(f32[75]{0:T(128)S(1)} %reshape.13.jac, s32[1,384]{1,0:T(1,128)S(1)} %reshape.14.cells, f32[5,4,32,128]{3,2,1,0:T(8,128)S(1)} %copy-done), custom_call_target="tpu_custom_call" | custom-call | tf_op jit(solution)/shard_map/stencil/pallas_call | solution.py:229
  51.2 1.8 %copy.14.history = f32[384,5,128]{2,1,0:T(8,128)S(1)} copy(f32[384,5,128]{2,0,1:T(8,128)} %param.9) | data formatting | bytes 1966080 | tf_op args[2]
  53.0 0.0 copy-done.1
  53.0 20.1 %radiate.1.value = f32[256,128]{1,0:T(8,128)S(1)} custom-call(f32[64,128]{1,0:T(8,128)S(1)} %copy-done.1, s32[1,384]{1,0:T(1,128)S(1)} %reshape.14.cells, s32[1]{0:T(128)} %bitcast.2.blocks, f32[256,3]{1,0:T(8,128)S(1)} %bitcast.3, f32[384,5,128]{2,1,0:T(8,128)S(1)} %copy.14.history, f32[3,8,384]{2,1,0:T(8,128)S(1)} %get-tuple-element.5.samples), custom_call_target="tpu_custom_call" | custom-call | tf_op jit(solution)/shard_map/radiate/pallas_call | solution.py:369
  73.1 18.4 %reduce.1 = f32[1,64]{1,0:T(1,128)S(1)} custom-call(f32[256,128]{1,0:T(8,128)S(1)} %radiate.1.value), custom_call_target="tpu_custom_call" | custom-call | tf_op jit(solution)/shard_map/reduce/pallas_call | solution.py:442
  91.5 0.7 copy.18
  92.2 0.5 copy.19
Async XLA Ops:
  0.6 52.3 %copy-start.1 = (f32[64,128]{1,0:T(8,128)S(1)}, f32[64,128]{1,0:T(8,128)}, u32[]{:S(2)}) copy-start(f32[64,128]{1,0:T(8,128)} %constant.2.clone.table) | copy-start | bytes 98308
  3.7 1.0 %copy-start = (f32[5,4,32,128]{3,2,1,0:T(8,128)S(1)}, f32[5,4,32,128]{3,2,1,0:T(8,128)}, u32[]{:S(2)}) copy-start(f32[5,4,32,128]{3,2,1,0:T(8,128)} %flow.1) | copy-start | bytes 983044

commit v2 on v0

v2 whole, which is shorter than its diff:
```python
import functools
import math

import jax
import jax.numpy as jnp
import numpy as np
from jax import lax
from jax.experimental import pallas as pl
from jax.experimental.pallas import tpu as pltpu
from jax.sharding import PartitionSpec as P

F32 = jnp.float32
MESH = pl.DeviceIdType.MESH
NV = 5
FREQ = 32
STEPS = 3
SURF_DEV = 128
TIME_STEP = 0.3
VISCOSITY = 0.05
PAD = 8
KEEP = (0.0, 0.75, 1.0 / 3.0)
GAIN = (1.0, 0.25, 2.0 / 3.0)
AXES = ("gx", "gz", "row")
OLD = (0, 5, 5, 5, 4, 4, 3, 3, 3)
NEW = ((0, 0, 0, 2, 4, 4, 0, 0, 0), (0, 0, 0, 0, 0, 0, 7, 8, 8))


def split_dot(left, right):
    total = None
    for _ in range(3):
        part = left.astype(jnp.bfloat16)
        left = left - part.astype(F32)
        piece = jnp.dot(part, right, preferred_element_type=F32)
        total = piece if total is None else total + piece
    return total


def poly(x, coefficients):
    total = jnp.full_like(x, coefficients[-1])
    for c in coefficients[-2::-1]:
        total = total * x + c
    return total


SIN = [(-1.0) ** n / math.factorial(2 * n + 1) for n in range(9)]
COS = [(-1.0) ** n / math.factorial(2 * n) for n in range(10)]


def fourier_table(samples):
    turns = np.arange(1, FREQ + 1)[:, None] * np.arange(samples)[None, :] % samples
    angles = 2.0 * np.pi * turns / samples
    return (np.concatenate([np.cos(angles), -np.sin(angles)]) / np.sqrt(samples)).astype(np.float32)


def turn_rows(samples):
    f = np.arange(1, FREQ + 1)
    zero = np.zeros(FREQ)

    def turned(factor, both):
        re, im = factor.real, factor.imag
        return [
            np.concatenate([re, re, re, re] if both else [re, re, zero, zero]),
            np.concatenate([-im, zero, -im, zero] if both else [-im, zero, zero, zero]),
            np.concatenate([zero, im, zero, im] if both else [zero, im, zero, zero]),
        ]

    last = samples - 1
    rows = turned(-1j * np.exp(2j * np.pi * f * last / samples), False)
    for t in range(STEPS - 1):
        rows += turned(np.exp(2j * np.pi * f * (STEPS - 1 - t) / samples), True)
    w = np.exp(-2j * np.pi * f * last / samples)
    rows += [
        np.concatenate([-w.imag, -w.imag, zero, zero]),
        np.concatenate([-w.real, w.imag / f, zero, zero]),
        np.concatenate([w.real / f, w.real / f, zero, zero]),
        np.concatenate([-w.imag / f, w.real, zero, zero]),
    ]
    rows += [np.zeros(128)] * (-len(rows) % 8)
    return np.stack(rows).astype(np.float32)


def whole_kernel(
    sizes, flow, cells_in, watch_in, blocks_in, jac_in, table_in, turns_in, history, field, out,
    U, cells, watch, blocks, jac, table, turns, held,
    xr, zs, zr, rs, rr, spec, samples, geo, tab, seats, line, value, got, rows, last,
    load_sem, send_sem, recv_sem, send1, recv1, send2, recv2,
):
    nx, nz, nr, cx, cz, cr = sizes
    grid = (nx * cx, nz * cz, nr * cr)
    plane = nz * nr
    slots = line.shape[1]
    groups = slots // 128
    times = held.shape[2]
    observers = watch.shape[1]
    tiles = observers // 8
    stages = 3 * STEPS
    index = [lax.axis_index(a) for a in AXES]
    counts = (nx, nz, nr)
    a, b, c = index
    seat = b * nr + c

    loads = [
        pltpu.make_async_copy(source, target, load_sem.at[n])
        for n, (source, target) in enumerate((
            (flow, U.at[0, :, :, pl.ds(PAD, cz), :]),
            (cells_in, cells), (watch_in, watch), (blocks_in, blocks),
            (jac_in, jac), (table_in, table), (turns_in, turns), (history, held),
        ))
    ]
    for x in loads:
        x.start()

    def along(d):
        return (lax.rem(a + d, nx), b, c)

    def across(d):
        other = lax.rem(seat + d, plane)
        return (a, other // nr, lax.rem(other, nr))

    barrier = pltpu.get_barrier_semaphore()
    for d in range(1, nx):
        pl.semaphore_signal(barrier, inc=1, device_id=along(d), device_id_type=MESH)
    for d in range(1, plane):
        pl.semaphore_signal(barrier, inc=1, device_id=across(d), device_id_type=MESH)

    there = [(index[axis] > 0, index[axis] < counts[axis] - 1) for axis in range(3)]

    def peer(axis, side):
        ids = list(index)
        ids[axis] = index[axis] + (1 if side else -1)
        return tuple(ids)

    for slot in range(3):
        for axis, buffer in enumerate((xr, zr, rr)):
            for side in range(2):
                @pl.when(jnp.logical_not(there[axis][side]))
                def _():
                    view = buffer.at[slot, side]
                    view[...] = jnp.zeros(view.shape, F32)

    for x in loads[1:3]:
        x.wait()
    for i in range(cells.shape[0]):
        line[0:1, 64 * i:64 * i + 64] = cells[i:i + 1, :]
    for d in range(3):
        for g in range(observers // 128):
            wide = jnp.broadcast_to(watch[d:d + 1, g * 128:g * 128 + 128], (128, 128))
            columns = wide.T
            for n in range(128 // plane):
                seats[d, pl.ds(g * (128 // plane) + n, plane, stride=nx), :] = columns[n * plane:(n + 1) * plane]

    lane = lax.broadcasted_iota(jnp.int32, (cz, cr), 1)
    lane8 = lax.broadcasted_iota(jnp.int32, (8, 128), 1)

    unit = 2.0 / grid[2]
    middle = 2.3
    norm = 1.0 / math.sqrt(nx * nz * nr * SURF_DEV)

    def geometry(i, carry):
        limit = blocks[0, 0] * 64
        span = pl.ds(pl.multiple_of(i * 32, 32), 32)
        at = (
            seats[0, span, :] * float(grid[0]),
            seats[1, span, :] * float(grid[1]),
            (1.25 + 0.75 * seats[2, span, :]) * float(grid[2]),
        )
        for g in range(groups):
            cols = slice(g * 128, (g + 1) * 128)
            spot = line[0:1, cols]
            place = (
                (index[0] * cx + spot // (cz * cr)).astype(F32) + 0.5,
                (index[1] * cz + spot // cr % cz).astype(F32) + 0.5,
                (index[2] * cr + spot % cr).astype(F32) + 0.5,
            )
            away = [at[d] - place[d] for d in range(3)]
            square = away[0] * away[0] + away[1] * away[1] + away[2] * away[2]
            distance = jnp.sqrt(square)
            inverse = 1.0 / distance
            for d in range(3):
                geo[d, span, cols] = away[d] * inverse
            geo[3, span, cols] = inverse * (1.0 / unit)
            angle = distance * unit - middle
            sq = angle * angle
            sine = angle * poly(sq, SIN)
            cosine = poly(sq, COS)
            cm, sm = math.cos(middle), math.sin(middle)
            step_r = cosine * cm - sine * sm
            step_i = -(sine * cm + cosine * sm)
            amp = jnp.where(lane + g * 128 < limit, inverse * (grid[2] * norm), 0.0)
            geo[4, span, cols] = step_r
            geo[5, span, cols] = step_i
            geo[6, span, cols] = amp * step_r
            geo[7, span, cols] = amp * step_i
        return carry

    def spectra():
        fourier = table[...]
        time = lax.broadcasted_iota(jnp.int32, fourier.shape, 1)
        early = jnp.where(time < times - STEPS, fourier, 0.0)
        for j in range(4):
            signal = held[j] + held[4] if j == 0 else held[j]
            spec[j] = lax.dot_general(
                early, signal, (((1,), (1,)), ((), ())),
                precision=lax.Precision.HIGHEST, preferred_element_type=F32,
            )

    def grow(step):
        at = times - STEPS + step
        for j in range(4):
            spec[j] = spec[j] + table[:, at:at + 1] * samples[step, j:j + 1, :]

    def turned(what, first):
        return (
            what * turns[first:first + 1, :]
            + pltpu.roll(what, 96, 1) * turns[first + 1:first + 2, :]
            + pltpu.roll(what, 32, 1) * turns[first + 2:first + 3, :]
        )

    def old_tile(i, carry):
        span = pl.ds(pl.multiple_of(i * 8, 8), 8)
        state = []
        for g in range(groups):
            state.append([geo[k, span, g * 128:(g + 1) * 128] for k in range(8)])
        result = jnp.zeros((8, 128), F32)
        for f in range(FREQ):
            real, imag = None, None
            for g in range(groups):
                cols = slice(g * 128, (g + 1) * 128)
                ex, ey, ez, near, zre, zim, ur, ui = state[g]
                tab[i, f, 0, :, cols] = ur
                tab[i, f, 1, :, cols] = ui
                sr = [spec[j, f:f + 1, cols] for j in range(4)]
                si = [spec[j, FREQ + f:FREQ + f + 1, cols] for j in range(4)]
                dr = ex * sr[1] + ey * sr[2] + ez * sr[3]
                di = ex * si[1] + ey * si[2] + ez * si[3]
                w = near * (1.0 / (f + 1))
                gr = w * dr - (si[0] + di)
                gi = w * di + (sr[0] + dr)
                pr = ur * gr - ui * gi
                pi = ur * gi + ui * gr
                real = pr if real is None else real + pr
                imag = pi if imag is None else imag + pi
                if f < FREQ - 1:
                    state[g][6] = ur * zre - ui * zim
                    state[g][7] = ur * zim + ui * zre
            result = jnp.where(lane8 == f, jnp.sum(real, axis=1, keepdims=True), result)
            result = jnp.where(lane8 == FREQ + f, jnp.sum(imag, axis=1, keepdims=True), result)
        value[span, :] = turned(result, 0)
        return carry

    def new_tile(i, t):
        span = pl.ds(pl.multiple_of(i * 8, 8), 8)
        weights = []
        for g in range(groups):
            cols = slice(g * 128, (g + 1) * 128)
            own = [samples[t, j:j + 1, cols] * (1.0 / math.sqrt(times)) for j in range(4)]
            dip = sum(geo[d, span, cols] * own[d + 1] for d in range(3))
            weights.append((own[0] + dip, geo[3, span, cols] * dip))
        what = jnp.zeros((8, 128), F32)
        for f in range(FREQ):
            phases = [[tab[i, f, n, :, g * 128:(g + 1) * 128] for n in range(2)] for g in range(groups)]
            for k in range(4):
                total = sum(weights[g][k // 2] * phases[g][k % 2] for g in range(groups))
                total = jnp.sum(total, axis=1, keepdims=True)
                what = jnp.where(lane8 == FREQ * k + f, total, what)
        return span, what

    def middle_tile(t, i, carry):
        span, what = new_tile(i, t)
        value[span, :] = value[span, :] + turned(what, 3 * (t + 1))
        return carry

    def last_tile(i, carry):
        span, what = new_tile(i, STEPS - 1)
        value[span, :] = value[span, :] + what
        return carry

    def fill(k):
        def upto(counts, i):
            return sum(jnp.where(i > n, count, 0) for n, count in enumerate(counts))

        for counts, act in (
            (OLD, old_tile), (NEW[0], functools.partial(middle_tile, 0)), (NEW[1], functools.partial(middle_tile, 1)),
        ):
            lax.fori_loop(upto(counts, k), upto(counts, k + 1), act, 0)

    def copy(axis, side, slot, mine):
        land = 1 - side if mine else side
        if axis == 0:
            src = U.at[slot, :, (cx - 1) if side else 0, pl.ds(PAD, cz), :]
            dst = xr.at[slot, land]
        elif axis == 1:
            src = zs.at[slot, side]
            dst = zr.at[slot, land]
        else:
            src = rs.at[slot]
            dst = rr.at[slot, land]
        return pltpu.make_async_remote_copy(
            src_ref=src, dst_ref=dst,
            send_sem=send_sem.at[axis, side, slot],
            recv_sem=recv_sem.at[axis, land, slot],
            device_id=peer(axis, side), device_id_type=MESH,
        )

    def for_sides(axis, act):
        for side in range(2):
            @pl.when(there[axis][side])
            def _():
                act(axis, side)

    def start_x(slot):
        for_sides(0, lambda axis, side: copy(axis, side, slot, True).start())

    def start_zr(slot):
        packed = jnp.zeros((cz, cr), F32)
        for v in range(NV):
            for x in range(cx):
                k = 2 * (v * cx + x)
                what = U[slot, v, x, PAD:PAD + cz, :]
                zs[slot, 0, v, x:x + 1, :] = what[:1]
                zs[slot, 1, v, x:x + 1, :] = what[cz - 1:]
                moved = pltpu.roll(what, k, 1) if k else what
                packed = jnp.where((lane == k) | (lane == (k - 1) % cr), moved, packed)
        rs[slot] = packed
        for axis in (2, 1):
            for_sides(axis, lambda axis, side: copy(axis, side, slot, True).start())

    def wait_received(slot):
        for axis in (1, 2, 0):
            for_sides(axis, lambda axis, side: copy(axis, side, slot, False).wait_recv())

    def wait_sent(slot):
        for axis in range(3):
            for_sides(axis, lambda axis, side: copy(axis, side, slot, True).wait_send())

    def pick(j, choices):
        return jnp.where(j == 0, choices[0], jnp.where(j == 1, choices[1], choices[2])).astype(F32)

    def stage(k):
        src, dst = lax.rem(k, 3), lax.rem(k + 1, 3)
        keep, gain = pick(src, KEEP), pick(src, GAIN)
        by_slope = gain * (0.5 * TIME_STEP)
        by_side = gain * (TIME_STEP * VISCOSITY)
        by_center = gain * (1.0 - 6.0 * VISCOSITY * TIME_STEP)
        for v in range(NV):
            for x in range(cx):
                U[src, v, x, PAD - 1:PAD, :] = zr[src, 0, v, x:x + 1, :]
                U[src, v, x, PAD + cz:PAD + cz + 1, :] = zr[src, 1, v, x:x + 1, :]
        halo = jnp.where(lane % 2 == 1, rr[src, 0], rr[src, 1])

        def layer(x):
            sums = [None] * NV
            rest = []
            for w in range(NV):
                center = U[src, w, x, PAD:PAD + cz, :]
                below = xr[src, 0, w] if x == 0 else U[src, w, x - 1, PAD:PAD + cz, :]
                above = xr[src, 1, w] if x == cx - 1 else U[src, w, x + 1, PAD:PAD + cz, :]
                before = U[src, w, x, PAD - 1:PAD + cz - 1, :]
                after = U[src, w, x, PAD + 1:PAD + cz + 1, :]
                n = 2 * (w * cx + x)
                moved = pltpu.roll(halo, cr - n, 1) if n else halo
                inner = pltpu.roll(jnp.where(lane == cr - 1, moved, center), 1, 1)
                outer = pltpu.roll(jnp.where(lane == 0, moved, center), cr - 1, 1)
                slopes = (above - below, after - before, outer - inner)
                beside = above + below + after + before + outer + inner
                rest.append(beside * by_side + center * by_center)
                for v in range(NV):
                    for d in range(3):
                        piece = slopes[d] * jac[v, d, w]
                        sums[v] = piece if sums[v] is None else sums[v] + piece
            for v in range(NV):
                what = sums[v] * by_slope + rest[v] + U[0, v, x, PAD:PAD + cz, :] * keep
                U[dst, v, x, PAD:PAD + cz, :] = what

        layer(0)
        layer(cx - 1)
        pl.when(k < stages - 1)(lambda: start_x(dst))
        for x in range(1, cx - 1):
            layer(x)

    height = lax.broadcasted_iota(jnp.int32, (cr, slots), 0)
    rows_of = lax.broadcasted_iota(jnp.int32, (cx * cz, slots), 0)

    def sample(step):
        spot = line[...]
        chosen_lane = jnp.where(height == spot % cr, 1.0, 0.0).astype(jnp.bfloat16)
        for j in range(4):
            tile = jnp.concatenate([U[0, j, x, PAD:PAD + cz, :] for x in range(cx)], axis=0)
            if j == 0:
                tile = tile + jnp.concatenate([U[0, 4, x, PAD:PAD + cz, :] for x in range(cx)], axis=0)
            picked = split_dot(tile, chosen_lane)
            picked = jnp.where(rows_of == spot // cr, picked, 0.0)
            picked = jnp.sum(picked, axis=0, keepdims=True)
            samples[step, j:j + 1, :] = picked

    loads[0].wait()
    pl.semaphore_wait(barrier, nx - 1 + plane - 1)
    start_x(0)

    def body(k, carry):
        slot = lax.rem(k, 3)
        start_zr(slot)

        @pl.when(k == 0)
        def _():
            for x in loads[3:]:
                x.wait()
            lax.fori_loop(0, observers // 32, geometry, 0)
            spectra()

        for step in range(STEPS - 1):
            @pl.when(k == 3 * step + 3)
            def _():
                sample(step)
                grow(step)

        fill(k)
        wait_received(slot)
        stage(k)
        wait_sent(slot)
        return carry

    lax.fori_loop(0, stages, body, 0)
    result = pltpu.make_async_copy(U.at[0, :, :, pl.ds(PAD, cz), :], field, load_sem.at[0])
    result.start()
    sample(STEPS - 1)

    def first(d):
        to = lax.rem(seat + d, plane)
        return pltpu.make_async_remote_copy(
            src_ref=value.at[pl.ds(pl.multiple_of(to * nx, nx), nx)],
            dst_ref=got.at[d - 1], send_sem=send1.at[d - 1], recv_sem=recv1.at[d - 1],
            device_id=across(d), device_id_type=MESH,
        )

    def second(d):
        to = lax.rem(a + d, nx)
        return pltpu.make_async_remote_copy(
            src_ref=rows.at[to], dst_ref=last.at[d - 1],
            send_sem=send2.at[d - 1], recv_sem=recv2.at[d - 1],
            device_id=along(d), device_id_type=MESH,
        )

    def chunk(d, carry):
        last_tile(lax.rem(seat + d, plane), 0)
        first(d).start()
        return carry

    lax.fori_loop(1, plane, chunk, 0)
    last_tile(seat, 0)
    total = value[pl.ds(pl.multiple_of(seat * nx, nx), nx)]
    for d in range(1, plane):
        first(d).wait_recv()
        total = total + got[d - 1]
    rows[...] = total[:, None, :]
    for d in range(1, nx):
        second(d).start()
    for d in range(1, nx):
        second(d).wait_recv()
    total = rows[a] + jnp.sum(last[...], axis=0)
    spectrum = total * turns[9:10, :]
    for n, shift in enumerate((96, 64, 32)):
        spectrum = spectrum + pltpu.roll(total, shift, 1) * turns[10 + n:11 + n, :]
    out[...] = spectrum[:, :2 * FREQ]
    for d in range(1, plane):
        first(d).wait_send()
    for d in range(1, nx):
        second(d).wait_send()
    result.wait()


def finish_kernel(field_in, spectrum_in, field, spectrum, held, line, sem):
    pairs = [(field_in.at[v], held.at[v], field.at[v]) for v in range(NV)]
    pairs.append((spectrum_in, line, spectrum))
    into = [pltpu.make_async_copy(p[0], p[1], sem.at[0, n]) for n, p in enumerate(pairs)]
    back = [pltpu.make_async_copy(p[1], p[2], sem.at[1, n]) for n, p in enumerate(pairs)]
    for x in into:
        x.start()
    for x, y in zip(into, back):
        x.wait()
        y.start()
    for y in back:
        y.wait()


def finish(field, spectrum):
    hbm = pl.BlockSpec(memory_space=pltpu.HBM)
    return pl.pallas_call(
        finish_kernel,
        out_shape=(
            jax.ShapeDtypeStruct(field.shape, F32),
            jax.ShapeDtypeStruct(spectrum.shape, F32),
        ),
        in_specs=[hbm, hbm],
        out_specs=(hbm, hbm),
        scratch_shapes=[
            pltpu.VMEM(field.shape, F32),
            pltpu.VMEM(spectrum.shape, F32),
            pltpu.SemaphoreType.DMA((2, NV + 1)),
        ],
        compiler_params=pltpu.CompilerParams(vmem_limit_bytes=63 << 20),
        name="finish",
    )(field, spectrum)


def solution(mesh):
    counts = tuple(mesh.shape[a] for a in AXES)
    nx, nz, nr = counts
    plane = nz * nr
    assert nx == 8

    def per_device(flow, jacobian, history, cell, blocks, observers):
        sizes = counts + flow.shape[1:]
        cx, cz, cr = flow.shape[1:]
        slots, times = history.shape[0], history.shape[2]
        seats = observers.shape[1]
        hbm = pl.BlockSpec(memory_space=pltpu.HBM)
        dma = pltpu.SemaphoreType.DMA
        lanes = turn_rows(times)
        field, spectrum = pl.pallas_call(
            functools.partial(whole_kernel, sizes),
            out_shape=(
                jax.ShapeDtypeStruct(flow.shape, F32),
                jax.ShapeDtypeStruct((1, 2 * FREQ), F32),
            ),
            in_specs=[hbm] * 8,
            out_specs=(hbm, pl.BlockSpec(memory_space=pltpu.VMEM)),
            scratch_shapes=[
                pltpu.VMEM((3, NV, cx, cz + 2 * PAD, cr), F32),
                pltpu.VMEM(cell.shape, jnp.int32),
                pltpu.VMEM(observers.shape, F32),
                pltpu.SMEM(blocks.shape, jnp.int32),
                pltpu.SMEM((NV, 3, NV), F32),
                pltpu.VMEM((2 * FREQ, times), F32),
                pltpu.VMEM(lanes.shape, F32),
                pltpu.VMEM((NV, slots, times), F32),
                pltpu.VMEM((3, 2, NV, cz, cr), F32),
                pltpu.VMEM((3, 2, NV, cx, cr), F32),
                pltpu.VMEM((3, 2, NV, cx, cr), F32),
                pltpu.VMEM((3, cz, cr), F32),
                pltpu.VMEM((3, 2, cz, cr), F32),
                pltpu.VMEM((4, 2 * FREQ, slots), F32),
                pltpu.VMEM((STEPS, 8, slots), F32),
                pltpu.VMEM((8, seats, slots), F32),
                pltpu.VMEM((seats // 8, FREQ, 2, 8, slots), F32),
                pltpu.VMEM((3, seats, 128), F32),
                pltpu.VMEM((1, slots), jnp.int32),
                pltpu.VMEM((seats, 128), F32),
                pltpu.VMEM((plane - 1, nx, 128), F32),
                pltpu.VMEM((nx, 1, 128), F32),
                pltpu.VMEM((nx - 1, 1, 128), F32),
                dma((8,)),
                dma((3, 2, 3)),
                dma((3, 2, 3)),
                dma((plane - 1,)),
                dma((plane - 1,)),
                dma((nx - 1,)),
                dma((nx - 1,)),
            ],
            compiler_params=pltpu.CompilerParams(
                collective_id=0, has_side_effects=True, vmem_limit_bytes=63 << 20
            ),
            name="whole",
        )(
            flow, cell, observers, blocks, jacobian.transpose(1, 0, 2),
            jnp.asarray(fourier_table(times)), jnp.asarray(lanes), history.transpose(1, 0, 2),
        )
        return finish(field, spectrum)

    return jax.shard_map(
        per_device,
        mesh=mesh,
        in_specs=(
            P(None, "gx", "gz", "row"),
            P(),
            P(AXES, None, None),
            P(AXES, None),
            P("row", ("gx", "gz")),
            P(),
        ),
        out_specs=(P(None, "gx", "gz", "row"), P(AXES, None)),
        check_vma=False,
    )
```

time: 421 us -> 72.7 us (0.17)
  the two profiles are of different devices: /device:TPU:32 before, /device:TPU:1 now
where the time goes in v2:
time: 72.7 us; the launch traced here: 72.4 us
  Pallas kernels  71.1 us (98%)
  between operations  1.29 us (2%)
    pallas_call x1, Pallas kernels, per_device(): pl.pallas_call(functools.partial(whole_kernel, sizes), out_shape=(jax.Sha...  69.4 us
    pallas_call x1, Pallas kernels, finish(): pl.pallas_call(finish_kernel, out_shape=(jax.ShapeDtypeStruct(field.shape...  1.7 us

profile of v2, /device:TPU:1, one launch (start us, length us, event | category | flops | bytes accessed | tf_op | source)
XLA Modules:
  0.0 72.4 jit_solution(1870243316503708938)
XLA Ops:
  1.3 69.4 %whole.1 = (f32[5,4,32,128]{3,2,1,0:T(8,128)}, f32[1,64]{1,0:T(1,128)}) custom-call(f32[5,4,32,128]{3,2,1,0:T(8,128)} %flow.1, s32[6,64]{1,0:T(8,128)} %cells_in.1, f32[3,256]{1,0:T(4,128)} %watch_in.1, s32[1,1]{1,0:T(1,128)S(6)} %copy.10.blocks_in, f32[5,3,5]{2,1,0:T(4,128)} %bitcast.3, f32[64,128]{1,0:T(8,128)} %constant.4.clone.table_in, ...), custom_call_target="tpu_custom_call" | custom-call | tf_op jit(solution)/shard_map/whole/pallas_call | solution.py:520
  70.7 1.7 %finish.1 = (f32[5,4,32,128]{3,2,1,0:T(8,128)}, f32[1,64]{1,0:T(1,128)}) custom-call(f32[5,4,32,128]{3,2,1,0:T(8,128)} %get-tuple-element.4.field_in, f32[1,64]{1,0:T(1,128)} %get-tuple-element.5.spectrum_in), custom_call_target="tpu_custom_call" | custom-call | tf_op jit(solution)/shard_map/finish/pallas_call | solution.py:488

commit v3 on v2

--- a/solution.py
+++ b/solution.py
@@ -21,8 +21,8 @@
 KEEP = (0.0, 0.75, 1.0 / 3.0)
 GAIN = (1.0, 0.25, 2.0 / 3.0)
 AXES = ("gx", "gz", "row")
-OLD = (0, 5, 5, 5, 4, 4, 3, 3, 3)
-NEW = ((0, 0, 0, 2, 4, 4, 0, 0, 0), (0, 0, 0, 0, 0, 0, 7, 8, 8))
+OLD = (0, 5, 5, 4, 4, 4, 3, 3, 4)
+NEW = ((0, 0, 0, 2, 4, 4, 0, 0, 0), (0, 0, 0, 0, 0, 0, 7, 8, 7))
 
 
 def split_dot(left, right):
@@ -99,6 +99,19 @@
     a, b, c = index
     seat = b * nr + c
 
+    def along(d):
+        return (lax.rem(a + d, nx), b, c)
+
+    def across(d):
+        other = lax.rem(seat + d, plane)
+        return (a, other // nr, lax.rem(other, nr))
+
+    barrier = pltpu.get_barrier_semaphore()
+    for d in range(1, nx):
+        pl.semaphore_signal(barrier, inc=1, device_id=along(d), device_id_type=MESH)
+    for d in range(1, plane):
+        pl.semaphore_signal(barrier, inc=1, device_id=across(d), device_id_type=MESH)
+
     loads = [
         pltpu.make_async_copy(source, target, load_sem.at[n])
         for n, (source, target) in enumerate((
@@ -110,19 +123,6 @@
     for x in loads:
         x.start()
 
-    def along(d):
-        return (lax.rem(a + d, nx), b, c)
-
-    def across(d):
-        other = lax.rem(seat + d, plane)
-        return (a, other // nr, lax.rem(other, nr))
-
-    barrier = pltpu.get_barrier_semaphore()
-    for d in range(1, nx):
-        pl.semaphore_signal(barrier, inc=1, device_id=along(d), device_id_type=MESH)
-    for d in range(1, plane):
-        pl.semaphore_signal(barrier, inc=1, device_id=across(d), device_id_type=MESH)
-
     there = [(index[axis] > 0, index[axis] < counts[axis] - 1) for axis in range(3)]
 
     def peer(axis, side):
@@ -138,16 +138,17 @@
                     view = buffer.at[slot, side]
                     view[...] = jnp.zeros(view.shape, F32)
 
-    for x in loads[1:3]:
-        x.wait()
-    for i in range(cells.shape[0]):
-        line[0:1, 64 * i:64 * i + 64] = cells[i:i + 1, :]
-    for d in range(3):
-        for g in range(observers // 128):
-            wide = jnp.broadcast_to(watch[d:d + 1, g * 128:g * 128 + 128], (128, 128))
-            columns = wide.T
-            for n in range(128 // plane):
-                seats[d, pl.ds(g * (128 // plane) + n, plane, stride=nx), :] = columns[n * plane:(n + 1) * plane]
+    def prepare():
+        for x in loads[1:3]:
+            x.wait()
+        for i in range(cells.shape[0]):
+            line[0:1, 64 * i:64 * i + 64] = cells[i:i + 1, :]
+        for d in range(3):
+            for g in range(observers // 128):
+                wide = jnp.broadcast_to(watch[d:d + 1, g * 128:g * 128 + 128], (128, 128))
+                columns = wide.T
+                for n in range(128 // plane):
+                    seats[d, pl.ds(g * (128 // plane) + n, plane, stride=nx), :] = columns[n * plane:(n + 1) * plane]
 
     lane = lax.broadcasted_iota(jnp.int32, (cz, cr), 1)
     lane8 = lax.broadcasted_iota(jnp.int32, (8, 128), 1)
@@ -325,9 +326,8 @@
         for axis in (2, 1):
             for_sides(axis, lambda axis, side: copy(axis, side, slot, True).start())
 
-    def wait_received(slot):
-        for axis in (1, 2, 0):
-            for_sides(axis, lambda axis, side: copy(axis, side, slot, False).wait_recv())
+    def wait_received(axis, slot):
+        for_sides(axis, lambda axis, side: copy(axis, side, slot, False).wait_recv())
 
     def wait_sent(slot):
         for axis in range(3):
@@ -342,6 +342,8 @@
         by_slope = gain * (0.5 * TIME_STEP)
         by_side = gain * (TIME_STEP * VISCOSITY)
         by_center = gain * (1.0 - 6.0 * VISCOSITY * TIME_STEP)
+        for axis in (1, 2):
+            wait_received(axis, src)
         for v in range(NV):
             for x in range(cx):
                 U[src, v, x, PAD - 1:PAD, :] = zr[src, 0, v, x:x + 1, :]
@@ -372,11 +374,14 @@
                 what = sums[v] * by_slope + rest[v] + U[0, v, x, PAD:PAD + cz, :] * keep
                 U[dst, v, x, PAD:PAD + cz, :] = what
 
-        layer(0)
-        layer(cx - 1)
-        pl.when(k < stages - 1)(lambda: start_x(dst))
         for x in range(1, cx - 1):
             layer(x)
+        pl.when(there[0][0])(lambda: copy(0, 0, src, False).wait_recv())
+        layer(0)
+        pl.when((k < stages - 1) & there[0][0])(lambda: copy(0, 0, dst, True).start())
+        pl.when(there[0][1])(lambda: copy(0, 1, src, False).wait_recv())
+        layer(cx - 1)
+        pl.when((k < stages - 1) & there[0][1])(lambda: copy(0, 1, dst, True).start())
 
     height = lax.broadcasted_iota(jnp.int32, (cr, slots), 0)
     rows_of = lax.broadcasted_iota(jnp.int32, (cx * cz, slots), 0)
@@ -403,6 +408,7 @@
 
         @pl.when(k == 0)
         def _():
+            prepare()
             for x in loads[3:]:
                 x.wait()
             lax.fori_loop(0, observers // 32, geometry, 0)
@@ -415,7 +421,6 @@
                 grow(step)
 
         fill(k)
-        wait_received(slot)
         stage(k)
         wait_sent(slot)
         return carry
@@ -429,7 +434,7 @@
         to = lax.rem(seat + d, plane)
         return pltpu.make_async_remote_copy(
             src_ref=value.at[pl.ds(pl.multiple_of(to * nx, nx), nx)],
-            dst_ref=got.at[d - 1], send_sem=send1.at[d - 1], recv_sem=recv1.at[d - 1],
+            dst_ref=got.at[d - 1], send_sem=send1.at[0], recv_sem=recv1.at[0],
             device_id=across(d), device_id_type=MESH,
         )
 
@@ -441,17 +446,22 @@
             device_id=along(d), device_id_type=MESH,
         )
 
-    def chunk(d, carry):
-        last_tile(lax.rem(seat + d, plane), 0)
-        first(d).start()
+    def chunk(n, carry):
+        pair = (2 * n + 1, 2 * n + 2)
+        for d in pair:
+            last_tile(lax.rem(seat + d, plane), 0)
+        first(pair[0]).start()
+        pl.when(pair[1] < plane)(lambda: first(pair[1]).start())
         return carry
 
-    lax.fori_loop(1, plane, chunk, 0)
-    last_tile(seat, 0)
+    lax.fori_loop(0, plane // 2, chunk, 0)
     total = value[pl.ds(pl.multiple_of(seat * nx, nx), nx)]
-    for d in range(1, plane):
-        first(d).wait_recv()
-        total = total + got[d - 1]
+    everything = pltpu.make_async_remote_copy(
+        src_ref=got, dst_ref=got, send_sem=send1.at[0], recv_sem=recv1.at[0],
+        device_id=across(1), device_id_type=MESH,
+    )
+    everything.wait_recv()
+    total = total + jnp.sum(got[...], axis=0)
     rows[...] = total[:, None, :]
     for d in range(1, nx):
         second(d).start()
@@ -462,8 +472,7 @@
     for n, shift in enumerate((96, 64, 32)):
         spectrum = spectrum + pltpu.roll(total, shift, 1) * turns[10 + n:11 + n, :]
     out[...] = spectrum[:, :2 * FREQ]
-    for d in range(1, plane):
-        first(d).wait_send()
+    everything.wait_send()
     for d in range(1, nx):
         second(d).wait_send()
     result.wait()
@@ -507,7 +516,7 @@
     counts = tuple(mesh.shape[a] for a in AXES)
     nx, nz, nr = counts
     plane = nz * nr
-    assert nx == 8
+    assert nx == 8 and plane == 32
 
     def per_device(flow, jacobian, history, cell, blocks, observers):
         sizes = counts + flow.shape[1:]
@@ -552,8 +561,8 @@
                 dma((8,)),
                 dma((3, 2, 3)),
                 dma((3, 2, 3)),
-                dma((plane - 1,)),
-                dma((plane - 1,)),
+                dma((1,)),
+                dma((1,)),
                 dma((nx - 1,)),
                 dma((nx - 1,)),
             ],

time: 72.7 us -> 70.2 us (0.966)
  Pallas kernels: 71.1 us -> 68.8 us
    pallas_call x1, Pallas kernels: 69.4 us -> 67.1 us  [per_device(): pl.pallas_call(functools.partial(whole_kernel, sizes), out_shape=(jax.Sha...]
where the time goes in v3:
time: 70.2 us; the launch traced here: 70.1 us
  Pallas kernels  68.8 us (98%)
  between operations  1.29 us (2%)
    pallas_call x1, Pallas kernels, per_device(): pl.pallas_call(functools.partial(whole_kernel, sizes), out_shape=(jax.Sha...  67.1 us
    pallas_call x1, Pallas kernels, finish(): pl.pallas_call(finish_kernel, out_shape=(jax.ShapeDtypeStruct(field.shape...  1.7 us

profile of v3, /device:TPU:1, one launch (start us, length us, event | category | flops | bytes accessed | tf_op | source)
XLA Modules:
  0.0 70.1 jit_solution(5585669794507799630)
XLA Ops:
  1.3 67.1 %whole.1 = (f32[5,4,32,128]{3,2,1,0:T(8,128)}, f32[1,64]{1,0:T(1,128)}) custom-call(f32[5,4,32,128]{3,2,1,0:T(8,128)} %flow.1, s32[6,64]{1,0:T(8,128)} %cells_in.1, f32[3,256]{1,0:T(4,128)} %watch_in.1, s32[1,1]{1,0:T(1,128)S(6)} %copy.10.blocks_in, f32[5,3,5]{2,1,0:T(4,128)} %bitcast.3, f32[64,128]{1,0:T(8,128)} %constant.4.clone.table_in, ...), custom_call_target="tpu_custom_call" | custom-call | tf_op jit(solution)/shard_map/whole/pallas_call | solution.py:529
  68.4 1.7 %finish.1 = (f32[5,4,32,128]{3,2,1,0:T(8,128)}, f32[1,64]{1,0:T(1,128)}) custom-call(f32[5,4,32,128]{3,2,1,0:T(8,128)} %get-tuple-element.4.field_in, f32[1,64]{1,0:T(1,128)} %get-tuple-element.5.spectrum_in), custom_call_target="tpu_custom_call" | custom-call | tf_op jit(solution)/shard_map/finish/pallas_call | solution.py:497

commit v4 on v3

--- a/solution.py
+++ b/solution.py
@@ -81,8 +81,8 @@
 
 def whole_kernel(
     sizes, flow, cells_in, watch_in, blocks_in, jac_in, table_in, turns_in, history, field, out,
-    U, cells, watch, blocks, jac, table, turns, held,
-    xr, zs, zr, rs, rr, spec, samples, geo, tab, seats, line, value, got, rows, last,
+    U, owed, cells, watch, blocks, jac, table, turns, held,
+    xs, xr, zs, zr, rs, rr, spec, samples, geo, tab, seats, line, value, got, rows, last,
     load_sem, send_sem, recv_sem, send1, recv1, send2, recv2,
 ):
     nx, nz, nr, cx, cz, cr = sizes
@@ -130,8 +130,9 @@
         ids[axis] = index[axis] + (1 if side else -1)
         return tuple(ids)
 
-    for slot in range(3):
-        for axis, buffer in enumerate((xr, zr, rr)):
+    owed[...] = jnp.zeros(owed.shape, F32)
+    for axis, buffer in enumerate((xr, zr, rr)):
+        for slot in range(buffer.shape[0]):
             for side in range(2):
                 @pl.when(jnp.logical_not(there[axis][side]))
                 def _():
@@ -288,7 +289,7 @@
     def copy(axis, side, slot, mine):
         land = 1 - side if mine else side
         if axis == 0:
-            src = U.at[slot, :, (cx - 1) if side else 0, pl.ds(PAD, cz), :]
+            src = xs.at[slot, side]
             dst = xr.at[slot, land]
         elif axis == 1:
             src = zs.at[slot, side]
@@ -329,8 +330,9 @@
     def wait_received(axis, slot):
         for_sides(axis, lambda axis, side: copy(axis, side, slot, False).wait_recv())
 
-    def wait_sent(slot):
+    def wait_sent(k):
         for axis in range(3):
+            slot = lax.rem(k, 3 if axis else 4)
             for_sides(axis, lambda axis, side: copy(axis, side, slot, True).wait_send())
 
     def pick(j, choices):
@@ -338,10 +340,28 @@
 
     def stage(k):
         src, dst = lax.rem(k, 3), lax.rem(k + 1, 3)
+        xsrc, xdst = lax.rem(k, 4), lax.rem(k + 1, 4)
         keep, gain = pick(src, KEEP), pick(src, GAIN)
         by_slope = gain * (0.5 * TIME_STEP)
         by_side = gain * (TIME_STEP * VISCOSITY)
         by_center = gain * (1.0 - 6.0 * VISCOSITY * TIME_STEP)
+        def across_face(values, side, slope, level):
+            added = []
+            for v in range(NV):
+                total = sum(values[w] * jac[v, 0, w] for w in range(NV)) * slope
+                added.append(values[v] * level + total if side else values[v] * level - total)
+            return added
+
+        old = lax.rem(k + 2, 3)
+        old_gain = pick(old, GAIN)
+        for side, x in ((0, 0), (1, cx - 1)):
+            @pl.when(there[0][side] & (k > 0))
+            def _():
+                mine = [U[old, w, x, PAD:PAD + cz, :] for w in range(NV)]
+                added = across_face(mine, 1 - side, old_gain * (0.5 * TIME_STEP), old_gain * (TIME_STEP * VISCOSITY))
+                for v in range(NV):
+                    owed[side, v] = added[v]
+
         for axis in (1, 2):
             wait_received(axis, src)
         for v in range(NV):
@@ -355,16 +375,22 @@
             rest = []
             for w in range(NV):
                 center = U[src, w, x, PAD:PAD + cz, :]
-                below = xr[src, 0, w] if x == 0 else U[src, w, x - 1, PAD:PAD + cz, :]
-                above = xr[src, 1, w] if x == cx - 1 else U[src, w, x + 1, PAD:PAD + cz, :]
+                below = None if x == 0 else U[src, w, x - 1, PAD:PAD + cz, :]
+                above = None if x == cx - 1 else U[src, w, x + 1, PAD:PAD + cz, :]
                 before = U[src, w, x, PAD - 1:PAD + cz - 1, :]
                 after = U[src, w, x, PAD + 1:PAD + cz + 1, :]
                 n = 2 * (w * cx + x)
                 moved = pltpu.roll(halo, cr - n, 1) if n else halo
                 inner = pltpu.roll(jnp.where(lane == cr - 1, moved, center), 1, 1)
                 outer = pltpu.roll(jnp.where(lane == 0, moved, center), cr - 1, 1)
-                slopes = (above - below, after - before, outer - inner)
-                beside = above + below + after + before + outer + inner
+                if below is None:
+                    slope, both = above, above
+                elif above is None:
+                    slope, both = -below, below
+                else:
+                    slope, both = above - below, above + below
+                slopes = (slope, after - before, outer - inner)
+                beside = both + after + before + outer + inner
                 rest.append(beside * by_side + center * by_center)
                 for v in range(NV):
                     for d in range(3):
@@ -372,16 +398,24 @@
                         sums[v] = piece if sums[v] is None else sums[v] + piece
             for v in range(NV):
                 what = sums[v] * by_slope + rest[v] + U[0, v, x, PAD:PAD + cz, :] * keep
-                U[dst, v, x, PAD:PAD + cz, :] = what
-
+                if x == 0:
+                    xs[xdst, 0, v] = what
+                elif x == cx - 1:
+                    xs[xdst, 1, v] = what
+                else:
+                    U[dst, v, x, PAD:PAD + cz, :] = what
+
+        for side, x in ((0, 0), (1, cx - 1)):
+            layer(x)
+            pl.when((k < stages - 1) & there[0][side])(lambda: copy(0, side, xdst, True).start())
         for x in range(1, cx - 1):
             layer(x)
-        pl.when(there[0][0])(lambda: copy(0, 0, src, False).wait_recv())
-        layer(0)
-        pl.when((k < stages - 1) & there[0][0])(lambda: copy(0, 0, dst, True).start())
-        pl.when(there[0][1])(lambda: copy(0, 1, src, False).wait_recv())
-        layer(cx - 1)
-        pl.when((k < stages - 1) & there[0][1])(lambda: copy(0, 1, dst, True).start())
+        for side, x in ((0, 0), (1, cx - 1)):
+            pl.when(there[0][side])(lambda: copy(0, side, xsrc, False).wait_recv())
+            theirs = [xr[xsrc, side, w] + owed[side, w] for w in range(NV)]
+            added = across_face(theirs, side, by_slope, by_side)
+            for v in range(NV):
+                U[dst, v, x, PAD:PAD + cz, :] = xs[xdst, side, v] + added[v]
 
     height = lax.broadcasted_iota(jnp.int32, (cr, slots), 0)
     rows_of = lax.broadcasted_iota(jnp.int32, (cx * cz, slots), 0)
@@ -400,6 +434,8 @@
 
     loads[0].wait()
     pl.semaphore_wait(barrier, nx - 1 + plane - 1)
+    for side in range(2):
+        xs[0, side] = U[0, :, (cx - 1) * side, PAD:PAD + cz, :]
     start_x(0)
 
     def body(k, carry):
@@ -422,7 +458,7 @@
 
         fill(k)
         stage(k)
-        wait_sent(slot)
+        wait_sent(k)
         return carry
 
     lax.fori_loop(0, stages, body, 0)
@@ -536,6 +572,7 @@
             out_specs=(hbm, pl.BlockSpec(memory_space=pltpu.VMEM)),
             scratch_shapes=[
                 pltpu.VMEM((3, NV, cx, cz + 2 * PAD, cr), F32),
+                pltpu.VMEM((2, NV, cz, cr), F32),
                 pltpu.VMEM(cell.shape, jnp.int32),
                 pltpu.VMEM(observers.shape, F32),
                 pltpu.SMEM(blocks.shape, jnp.int32),
@@ -543,7 +580,8 @@
                 pltpu.VMEM((2 * FREQ, times), F32),
                 pltpu.VMEM(lanes.shape, F32),
                 pltpu.VMEM((NV, slots, times), F32),
-                pltpu.VMEM((3, 2, NV, cz, cr), F32),
+                pltpu.VMEM((4, 2, NV, cz, cr), F32),
+                pltpu.VMEM((4, 2, NV, cz, cr), F32),
                 pltpu.VMEM((3, 2, NV, cx, cr), F32),
                 pltpu.VMEM((3, 2, NV, cx, cr), F32),
                 pltpu.VMEM((3, cz, cr), F32),
@@ -559,8 +597,8 @@
                 pltpu.VMEM((nx, 1, 128), F32),
                 pltpu.VMEM((nx - 1, 1, 128), F32),
                 dma((8,)),
-                dma((3, 2, 3)),
-                dma((3, 2, 3)),
+                dma((3, 2, 4)),
+                dma((3, 2, 4)),
                 dma((1,)),
                 dma((1,)),
                 dma((nx - 1,)),

time: 70.2 us -> 69.1 us (0.984)
  Pallas kernels: 68.8 us -> 67.7 us
    pallas_call x1, Pallas kernels: 67.1 us -> 66 us  [per_device(): pl.pallas_call(functools.partial(whole_kernel, sizes), out_shape=(jax.Sha...]
where the time goes in v4:
time: 69.1 us; the launch traced here: 68.9 us
  Pallas kernels  67.7 us (98%)
  between operations  1.29 us (2%)
    pallas_call x1, Pallas kernels, per_device(): pl.pallas_call(functools.partial(whole_kernel, sizes), out_shape=(jax.Sha...  66 us
    pallas_call x1, Pallas kernels, finish(): pl.pallas_call(finish_kernel, out_shape=(jax.ShapeDtypeStruct(field.shape...  1.7 us

profile of v4, /device:TPU:1, one launch (start us, length us, event | category | flops | bytes accessed | tf_op | source)
XLA Modules:
  0.0 68.9 jit_solution(7607929230972291804)
XLA Ops:
  1.3 66.0 %whole.1 = (f32[5,4,32,128]{3,2,1,0:T(8,128)}, f32[1,64]{1,0:T(1,128)}) custom-call(f32[5,4,32,128]{3,2,1,0:T(8,128)} %flow.1, s32[6,64]{1,0:T(8,128)} %cells_in.1, f32[3,256]{1,0:T(4,128)} %watch_in.1, s32[1,1]{1,0:T(1,128)S(6)} %copy.10.blocks_in, f32[5,3,5]{2,1,0:T(4,128)} %bitcast.3, f32[64,128]{1,0:T(8,128)} %constant.4.clone.table_in, ...), custom_call_target="tpu_custom_call" | custom-call | tf_op jit(solution)/shard_map/whole/pallas_call | solution.py:565
  67.2 1.7 %finish.1 = (f32[5,4,32,128]{3,2,1,0:T(8,128)}, f32[1,64]{1,0:T(1,128)}) custom-call(f32[5,4,32,128]{3,2,1,0:T(8,128)} %get-tuple-element.4.field_in, f32[1,64]{1,0:T(1,128)} %get-tuple-element.5.spectrum_in), custom_call_target="tpu_custom_call" | custom-call | tf_op jit(solution)/shard_map/finish/pallas_call | solution.py:533

commit v5 on v4

--- a/solution.py
+++ b/solution.py
@@ -22,7 +22,7 @@
 GAIN = (1.0, 0.25, 2.0 / 3.0)
 AXES = ("gx", "gz", "row")
 OLD = (0, 5, 5, 4, 4, 4, 3, 3, 4)
-NEW = ((0, 0, 0, 2, 4, 4, 0, 0, 0), (0, 0, 0, 0, 0, 0, 7, 8, 7))
+NEW = ((0, 0, 0, 2, 4, 4, 0, 0, 0), (0, 0, 0, 0, 0, 0, 6, 8, 8))
 
 
 def split_dot(left, right):
@@ -277,14 +277,19 @@
         value[span, :] = value[span, :] + what
         return carry
 
+    def middle_pair(t, n, carry):
+        middle_tile(t, 2 * n, 0)
+        middle_tile(t, 2 * n + 1, 0)
+        return carry
+
     def fill(k):
         def upto(counts, i):
             return sum(jnp.where(i > n, count, 0) for n, count in enumerate(counts))
 
-        for counts, act in (
-            (OLD, old_tile), (NEW[0], functools.partial(middle_tile, 0)), (NEW[1], functools.partial(middle_tile, 1)),
-        ):
-            lax.fori_loop(upto(counts, k), upto(counts, k + 1), act, 0)
+        lax.fori_loop(upto(OLD, k), upto(OLD, k + 1), old_tile, 0)
+        for t in range(STEPS - 1):
+            pairs = [count // 2 for count in NEW[t]]
+            lax.fori_loop(upto(pairs, k), upto(pairs, k + 1), functools.partial(middle_pair, t), 0)
 
     def copy(axis, side, slot, mine):
         land = 1 - side if mine else side

time: 69.1 us -> 68 us (0.984)
  Pallas kernels: 67.7 us -> 66.6 us
    pallas_call x1, Pallas kernels: 66 us -> 64.9 us  [per_device(): pl.pallas_call(functools.partial(whole_kernel, sizes), out_shape=(jax.Sha...]
where the time goes in v5:
time: 68 us; the launch traced here: 67.9 us
  Pallas kernels  66.6 us (98%)
  between operations  1.29 us (2%)
    pallas_call x1, Pallas kernels, per_device(): pl.pallas_call(functools.partial(whole_kernel, sizes), out_shape=(jax.Sha...  64.9 us
    pallas_call x1, Pallas kernels, finish(): pl.pallas_call(finish_kernel, out_shape=(jax.ShapeDtypeStruct(field.shape...  1.7 us

profile of v5, /device:TPU:1, one launch (start us, length us, event | category | flops | bytes accessed | tf_op | source)
XLA Modules:
  0.0 67.9 jit_solution(8506302013901833819)
XLA Ops:
  1.3 64.9 %whole.1 = (f32[5,4,32,128]{3,2,1,0:T(8,128)}, f32[1,64]{1,0:T(1,128)}) custom-call(f32[5,4,32,128]{3,2,1,0:T(8,128)} %flow.1, s32[6,64]{1,0:T(8,128)} %cells_in.1, f32[3,256]{1,0:T(4,128)} %watch_in.1, s32[1,1]{1,0:T(1,128)S(6)} %copy.10.blocks_in, f32[5,3,5]{2,1,0:T(4,128)} %bitcast.3, f32[64,128]{1,0:T(8,128)} %constant.4.clone.table_in, ...), custom_call_target="tpu_custom_call" | custom-call | tf_op jit(solution)/shard_map/whole/pallas_call | solution.py:570
  66.2 1.7 %finish.1 = (f32[5,4,32,128]{3,2,1,0:T(8,128)}, f32[1,64]{1,0:T(1,128)}) custom-call(f32[5,4,32,128]{3,2,1,0:T(8,128)} %get-tuple-element.4.field_in, f32[1,64]{1,0:T(1,128)} %get-tuple-element.5.spectrum_in), custom_call_target="tpu_custom_call" | custom-call | tf_op jit(solution)/shard_map/finish/pallas_call | solution.py:538
